TPU v7x, 256 devices: a whole 4x4x8 slice. The times are simulated.
256 devices in a mesh: seq: 32 (over z, x_lo, core), mp: 8 (over y, x_hi).
Axes of the slice: x: 4 (x_hi: 2, x_lo: 2; x = x_hi * 2 + x_lo), y: 4, z: 8, core: 2. Of those that a mesh axis runs over, the one named last changes fastest.
Arguments:
- streams: float32 [4096, 3, 4096], P('seq', None, 'mp'), may hold values from -6 to 6
- se_filter: float32 [7, 3, 256], P(None, None, 'mp'), may hold values from -3 to 3
- mr_filter: float32 [128, 256], P(None, 'mp'), may hold values from -1.5 to 1.5
- mr_decay: float32 [256], P('mp'), may hold values from 0.004 to 0.1
- query: float32 [4096, 4096], P('seq', 'mp'), may hold values from -8 to 8
- key: float32 [4096, 4096], P('seq', 'mp'), may hold values from -8 to 8
- value: float32 [4096, 4096], P('seq', 'mp'), may hold values from -6 to 6
- placement_list: int32 [32], replicated, may hold values from 0 to 31, each once
- doc_ids: int32 [4096], replicated, may hold values from 0 to 7, never falling along the last dimension, each value on 1 to 1024 neighbouring positions
- norm_gain: float32 [4096], P('mp'), may hold values from 0.25 to 1.75
Outputs:
- mixed: float32 [4096, 4096], P('seq', 'mp')
Inputs may be any that keep to these rules, and one draw needn't show every extreme that they name: placement_list names every stretch once. doc_ids never falls along the sequence; each document holds at most 1024 positions and one holds exactly that many.
All inputs are finite; a program needn't handle non-finite values.
Results may differ from a plain program's by a relative error of at most 0.0003.
Values sent between devices are 32-bit elements; how exact they have to be, the bound alone decides.
No kernel may reach another device: no remote copies, remote signals or barrier semaphores. Data moves between devices by JAX's collectives and lax.ppermute only.
A program may use at most 128 MiB of HBM per device.

v0:
```python
import jax
import jax.numpy as jnp
from jax import lax
from jax.experimental import pallas as pl
from jax.experimental.pallas import tpu as pltpu
from jax.sharding import PartitionSpec as P


N = 32
T = 128
HD = 128
W = 512
NB = 9
SE = 7
FAR = 27
VMEM = pl.BlockSpec(memory_space=pltpu.VMEM)
SMEM = pl.BlockSpec(memory_space=pltpu.SMEM)
ANY = pl.BlockSpec(memory_space=pl.ANY)
HIGHEST = lax.Precision.HIGHEST
F32 = jnp.float32


def hbm(x):
    return pltpu.with_memory_space_constraint(x, pltpu.HBM)


def vmem(x):
    return pltpu.with_memory_space_constraint(x, pltpu.VMEM)


def iota(shape, dim):
    return lax.broadcasted_iota(jnp.int32, shape, dim)


def column(row):
    eye = iota((T, T), 0) == iota((T, T), 1)
    return jnp.sum(jnp.where(eye, row, 0.0), axis=1, keepdims=True)


def doc_row(doc_ref, stretch):
    row = doc_ref[pl.ds(jnp.maximum(stretch, 0), 1), :].astype(F32)
    return jnp.where(stretch >= 0, row, -1.0)


def expand():
    return jnp.where(iota((32, W), 1) // 16 == iota((32, W), 0), 1.0, 0.0)


def fill_inverse(place_ref, inv_ref):
    for b in range(N):
        inv_ref[place_ref[b]] = b


def pack_kernel(q_ref, k_ref, v_ref, *outs):
    zq = lax.axis_index("seq") // 8
    for k, out in enumerate(outs):
        head = lax.rem(zq + k, 4)
        lanes = pl.ds(pl.multiple_of(head * HD, HD), HD)
        for t, ref in enumerate((q_ref, k_ref, v_ref)):
            out[t] = ref[:, lanes]


def local_kernel(place_ref, doc_ref, st_ref, se_ref, p_ref, f0_ref, g_ref, h_ref, short_ref, x_ref):
    c = place_ref[lax.axis_index("seq")]
    row = doc_row(doc_ref, c)
    col = column(row)
    earlier = (row == col) & (iota((T, T), 1) < iota((T, T), 0))
    run = jnp.broadcast_to(jnp.sum(jnp.where(earlier, 1.0, 0.0), axis=1, keepdims=True), (T, T))
    ex = expand()
    x_ref[:, 0:8, :] = jnp.zeros((3, 8, W), F32)
    x_ref[:, 8:, :] = st_ref[...]
    taps = [jnp.dot(se_ref[j], ex, precision=HIGHEST, preferred_element_type=F32) for j in range(3)]
    for j in range(3):
        short_ref[j] = taps[j]
    for lane in range(4):
        ls = slice(lane * 128, lane * 128 + 128)
        feats = []
        for j in range(3):
            acc = x_ref[j, 8:, ls] * taps[j][0:1, ls]
            for lag in range(1, SE):
                acc = acc + jnp.where(
                    run >= lag, x_ref[j, 8 - lag : 8 + T - lag, ls] * taps[j][lag : lag + 1, ls], 0.0
                )
            feats.append(acc)
        f0_ref[:, ls] = feats[0]
        gated = feats[1] * feats[2]
        g_ref[:, ls] = gated
        for r in range(15):
            p_ref[r * 4 + lane] = gated[8 * r + 8 : 8 * r + 16]
        for j in (1, 2):
            h_ref[j - 1, :, ls] = feats[j][0:8]
            p_ref[(14 + j) * 4 + lane] = feats[j][0:8]
            p_ref[77 + j * 4 + lane] = st_ref[j, T - 8 :, ls]
        for j in range(3):
            p_ref[(17 + j) * 4 + lane] = st_ref[j, T - 8 :, ls]
    p_ref[80] = jnp.zeros((8, 128), F32)
    p_ref[89:96] = jnp.zeros((7, 8, 128), F32)


def select_kernel(place_ref, r_ref, s_ref, inv_ref):
    fill_inverse(place_ref, inv_ref)
    back = jnp.where(lax.axis_index("seq") < FAR, 1, 2)
    for d in range(N):
        s_ref[d] = r_ref[inv_ref[jnp.maximum(place_ref[d] - back, 0)]]


def halo(tail, taps, run):
    acc = jnp.zeros_like(tail)
    rows = iota(tail.shape, 0)
    for lag in range(1, SE):
        linked = (rows < lag) & (run >= lag)
        acc = acc + jnp.where(linked, pltpu.roll(tail, lag, 0) * taps[lag : lag + 1], 0.0)
    return acc


def long_taps(mr_ref, decay_ref, ex):
    small = iota((32, 32), 0) == iota((32, 32), 1)
    decay = jnp.sum(jnp.where(small, decay_ref[...], 0.0), axis=1, keepdims=True)
    taps = mr_ref[...] * jnp.exp(-decay * iota((32, T), 1).astype(F32))
    return lax.dot_general(taps, ex, (((0,), (0,)), ((), ())), precision=HIGHEST, preferred_element_type=F32)


def run_of(rows, own, prev):
    same = jnp.sum(jnp.where(prev == rows, 1.0, 0.0), axis=1, keepdims=True)
    at = iota((rows.shape[0], T), 0)
    earlier = (own == rows) & (iota((rows.shape[0], T), 1) < at)
    return same + jnp.sum(jnp.where(earlier, 1.0, 0.0), axis=1, keepdims=True)


def convolve(e_ref, s_ref, t_ref, run_ref, span, plain, masked, keep, write):
    for r in range(8):
        s_ref[r, span[0] : span[1], :] = e_ref[span[0] - r : span[1] - r, :]

    def lane_tile(lane, _):
        ls = pl.ds(pl.multiple_of(lane * 128, 128), 128)
        acc = [jnp.zeros((8, 128), F32) for _ in range(16)]

        def terms(blocks, mask):
            for m in range(16):
                if not len(blocks(m)):
                    continue
                rows = t_ref[8 * m : 8 * m + 8, ls]
                for r in range(8):
                    tap = jnp.broadcast_to(rows[r : r + 1], (8, 128))
                    for i in blocks(m):
                        first = T - 8 * m + 8 * i
                        term = s_ref[r, first : first + 8, ls] * tap
                        if mask:
                            term = jnp.where(run_ref[8 * i : 8 * i + 8, :] >= 8 * m + r, term, 0.0)
                        acc[i] = acc[i] + term

        if keep is not None:
            terms(plain, False)
            for i in range(16):
                acc[i] = jnp.where(keep(i), acc[i], 0.0)
        terms(masked, True)
        write(ls, acc)
        return 0

    lax.fori_loop(0, 4, lane_tile, 0)


def own_kernel(place_ref, doc_ref, mr_ref, decay_ref, g_ref, out_ref, t_ref, e_ref, s_ref, run_ref):
    c = place_ref[lax.axis_index("seq")]
    row = doc_row(doc_ref, c)
    run_ref[...] = jnp.broadcast_to(run_of(column(row), row, doc_row(doc_ref, c - 1)), (T, T))
    t_ref[...] = long_taps(mr_ref, decay_ref, expand())
    e_ref[T : T + 8, :] = jnp.zeros((8, W), F32)
    e_ref[T + 8 :, :] = g_ref[8:, :]

    def write(ls, acc):
        for i in range(16):
            out_ref[8 * i : 8 * i + 8, ls] = acc[i]

    convolve(e_ref, s_ref, t_ref, run_ref, (T + 8, 2 * T), None, lambda m: range(m + 1, 16), None, write)


def halo_kernel(
    place_ref, doc_ref, short_ref, t_ref, f0_ref, own_ref, h_ref, p_ref, out_ref, e_ref, s_ref, run_ref, first_ref
):
    c = place_ref[lax.axis_index("seq")]
    row, before, before2 = (doc_row(doc_ref, c - i) for i in range(3))
    run = jnp.broadcast_to(run_of(column(row), row, before), (T, T))
    run_ref[...] = run
    run8 = jnp.broadcast_to(run[0:8, 0:1], (8, W))
    prev8 = jnp.broadcast_to(run_of(column(before)[0:8], before, before2), (8, W))
    short = [short_ref[j] for j in range(3)]
    start = row[:, 0:1]
    first_ref[...] = jnp.broadcast_to(jnp.where(column(row) == start, 1.0, 0.0), (T, T))
    linked = jnp.where(column(before) == start, 1.0, 0.0)

    def rows_of(first):
        return jnp.concatenate([p_ref[first + lane] for lane in range(4)], axis=1)

    own = [h_ref[j - 1] + halo(rows_of((17 + j) * 4), short[j], run8) for j in (1, 2)]
    prev = [rows_of((14 + j) * 4) + halo(rows_of(77 + j * 4), short[j], prev8) for j in (1, 2)]
    e_ref[0:8, :] = jnp.where(linked[0:8] > 0.0, prev[0] * prev[1], 0.0)
    for r in range(15):
        rows = slice(8 * r + 8, 8 * r + 16)
        e_ref[rows, :] = jnp.where(linked[rows] > 0.0, rows_of(r * 4), 0.0)
    e_ref[T : T + 8, :] = own[0] * own[1]
    e_ref[T + 8 : T + 16, :] = jnp.zeros((8, W), F32)
    out_ref[0:8, :] = f0_ref[0:8, :] + halo(rows_of(68), short[0], run8)
    out_ref[8:, :] = f0_ref[8:, :]

    def write(ls, acc):
        for i in range(16):
            rows = slice(8 * i, 8 * i + 8)
            out_ref[rows, ls] = out_ref[rows, ls] * (own_ref[rows, ls] + acc[i])

    def keep(i):
        return first_ref[8 * i : 8 * i + 8, :] > 0.0

    convolve(
        e_ref, s_ref, t_ref, run_ref, (8, T + 16), lambda m: range(0, m), lambda m: range(m, min(16, m + 2)), keep, write
    )


def split(x):
    high = x.astype(jnp.bfloat16)
    return high, (x - high.astype(F32)).astype(jnp.bfloat16)


def dot3(a, high, low, dims):
    def dot(x, y):
        return lax.dot_general(x, y, (dims, ((), ())), preferred_element_type=F32)

    both = dot(a, high)
    return both[:T] + (both[T:] + dot(a[:T], low))


def attend_kernel(
    place_ref, doc_ref, a0, a1, a2, a3, *rest
):
    kv, rest = rest[:16], rest[16:]
    outs, (q_ref, kv_ref, sem, kh, kl, vh, vl, s_ref, qs_ref, p_ref) = rest[:4], rest[4:]
    copies = []

    def fetch(src, dst):
        copies.append(pltpu.make_async_copy(src, dst, sem.at[len(copies)]))
        copies[-1].start()

    for n, ref in enumerate(kv):
        fetch(ref, kv_ref.at[n // 2, n % 2])
    for i, ref in enumerate((a0, a1, a2, a3)):
        fetch(ref.at[0], q_ref.at[i])
    me = lax.axis_index("seq")
    zq = me // 8
    g = lax.rem(me, 8)

    for x in range(8):
        copies[2 * x].wait()
        copies[2 * x + 1].wait()
        for k in range(4):
            at = place_ref[lax.rem(zq + 4 - k, 4) * 8 + lax.bitwise_xor(g, x)]
            rows = pl.ds(pl.multiple_of(at * T, T), T)
            kh[rows, :], kl[rows, :] = split(kv_ref[x, 0, k])
            vh[rows, :], vl[rows, :] = split(kv_ref[x, 1, k])
    for copy in copies[16:]:
        copy.wait()
    scale = 1.0 / jnp.sqrt(jnp.float32(HD))
    ahead = iota((T, T), 1) - iota((T, T), 0)
    for i in range(4):
        c = place_ref[lax.rem(zq + 4 - i, 4) * 8 + g]
        first = jnp.maximum(c - (NB - 1), 0)
        col = column(doc_row(doc_ref, c))
        qs_ref[:T, :], qs_ref[T:, :] = split(q_ref[i])
        rows = pl.ds(pl.multiple_of(first * T, T), NB * T)
        s_ref[...] = dot3(qs_ref[...], kh[rows, :], kl[rows, :], ((1,), (1,))) * scale
        top = None
        for n in range(NB):
            cols = slice(n * T, n * T + T)
            allowed = (doc_row(doc_ref, first + n) == col) & (ahead <= (c - first - n) * T)
            s = jnp.where(allowed, s_ref[:, cols], -1e30)
            s_ref[:, cols] = s
            top = s if top is None else jnp.maximum(top, s)
        top = jnp.max(top, axis=1, keepdims=True)
        total = jnp.zeros((T, T), F32)
        for n in range(NB):
            cols = slice(n * T, n * T + T)
            p = jnp.exp(s_ref[:, cols] - top)
            total = total + p
            p_ref[:T, cols], p_ref[T:, cols] = split(p)
        acc = dot3(p_ref[...], vh[rows, :], vl[rows, :], ((1,), (0,)))
        outs[i][...] = acc / jnp.sum(total, axis=1, keepdims=True)


def join_kernel(hy_ref, a0, a1, a2, a3, out_ref, sq_ref):
    zq = lax.axis_index("seq") // 8
    for k, ref in enumerate((a0, a1, a2, a3)):
        lanes = pl.ds(pl.multiple_of(lax.rem(zq + k, 4) * HD, HD), HD)
        out_ref[:, lanes] = hy_ref[:, lanes] + ref[...]
    y = out_ref[...]
    sq_ref[...] = lax.dot_general(
        jnp.ones((8, W), F32), y * y, (((1,), (1,)), ((), ())), precision=HIGHEST, preferred_element_type=F32
    )


def norm_kernel(y_ref, sq_ref, other_ref, gain_ref, out_ref):
    mean = column(sq_ref[0:1, :] + other_ref[0:1, :]) / (8.0 * W)
    out_ref[...] = y_ref[...] * lax.rsqrt(mean + 1e-05) * gain_ref[...]


def call(kernel, out, ins, scratch=()):
    shapes = [jax.ShapeDtypeStruct(s, F32) for s in out]
    one = len(shapes) == 1
    return pl.pallas_call(
        kernel,
        out_shape=shapes[0] if one else shapes,
        in_specs=ins,
        out_specs=VMEM if one else [VMEM] * len(shapes),
        scratch_shapes=scratch,
    )


def per_device(streams, se_filter, mr_filter, mr_decay, query, key, value, placement_list, doc_ids, norm_gain):
    st = streams.transpose(1, 0, 2)
    se = se_filter.transpose(1, 0, 2)
    mr = mr_filter.T
    docs = doc_ids.reshape(N, T)

    def ring(x, k):
        return lax.ppermute(x, "seq", [(b, (b + 8 * k) % N) for b in range(N)])

    def swap(x, axis, bit):
        return lax.ppermute(x, axis, [(b, b ^ bit) for b in range(N if axis == "seq" else 8)])

    packed = call(pack_kernel, [(3, T, HD)] * 4, [VMEM] * 3)(query, key, value)
    held = [packed[0]] + [None] * 3
    for k in (2, 1, 3):
        held[k] = ring(packed[k], k)

    tiles, f0, gated, heads, short = call(
        local_kernel,
        [(96, 8, 128), (T, W), (T, W), (2, 8, W), (3, SE, W)],
        [SMEM, VMEM, VMEM, VMEM],
        [pltpu.VMEM((3, T + 8, W), F32)],
    )(placement_list, docs, st, se)
    pieces = lax.all_to_all(tiles.reshape(N, 24, 128), "seq", 0, 0, tiled=True)
    conv = [pltpu.VMEM((256, W), F32), pltpu.VMEM((8, 256, W), F32), pltpu.VMEM((T, T), F32)]
    decay = mr_decay.reshape(1, 32)
    own, taps = call(own_kernel, [(T, W), (T, W)], [SMEM] + [VMEM] * 4, conv)(placement_list, docs, mr, decay, gated)

    k0, v0 = (jnp.concatenate([a[t : t + 1] for a in held], axis=0) for t in (1, 2))
    zk = swap(k0, "seq", 4)
    xv = swap(v0, "seq", 2)
    zv = swap(v0, "seq", 4)
    xk = swap(k0, "seq", 2)
    dk = swap(zk, "seq", 2)
    dv = swap(xv, "seq", 4)
    ck, cv, cxk, cxv, czk, czv, cdk, cdv = (
        swap(a, "seq", 1) for a in (k0, v0, xk, xv, zk, zv, dk, dv)
    )

    chosen = call(select_kernel, [(N, 24, 128)], [SMEM, VMEM], [pltpu.SMEM((N,), jnp.int32)])(
        placement_list, hbm(pieces)
    )
    back = lax.all_to_all(chosen, "seq", 0, 0, tiled=True).reshape(96, 8, 128)

    bf = jnp.bfloat16
    pieces_kv = (k0, v0, ck, cv, xk, xv, cxk, cxv, zk, zv, czk, czv, dk, dv, cdk, cdv)
    near = [hbm(a) for a in (*held[1:], *pieces_kv)]
    attended = call(
        attend_kernel,
        [(T, HD)] * 4,
        [SMEM, VMEM] + [ANY] * 20,
        [
            pltpu.VMEM((4, T, HD), F32),
            pltpu.VMEM((8, 2, 4, T, HD), F32),
            pltpu.SemaphoreType.DMA((20,)),
            *[pltpu.VMEM((N * T, HD), bf)] * 4,
            pltpu.VMEM((T, NB * T), F32),
            pltpu.VMEM((2 * T, HD), bf),
            pltpu.VMEM((2 * T, NB * T), bf),
        ],
    )(placement_list, docs, held[0], *near)
    home = [attended[0]] + [None] * 3
    for k in (2, 1, 3):
        home[k] = ring(attended[k], -k)

    hyena = call(halo_kernel, [(T, W)], [SMEM] + [VMEM] * 7, [*conv, pltpu.VMEM((T, T), F32)])(
        placement_list, docs, short, taps, f0, own, heads, vmem(back)
    )
    summed, squares = call(join_kernel, [(T, W), (8, 128)], [VMEM] * 5)(hyena, home[0], *map(vmem, home[1:]))

    def along_y(k):
        return lax.ppermute(squares, "mp", [(m, (m + 2 * k) % 8) for m in range(8)])

    squares = squares + along_y(2) + (along_y(1) + along_y(3))
    other = swap(squares, "mp", 1)
    return call(norm_kernel, [(T, W)], [VMEM] * 4)(summed, squares, vmem(other), norm_gain.reshape(1, W))


def solution(mesh):
    placed = (
        P("seq", None, "mp"),
        P(None, None, "mp"),
        P(None, "mp"),
        P("mp"),
        P("seq", "mp"),
        P("seq", "mp"),
        P("seq", "mp"),
        P(),
        P(),
        P("mp"),
    )
    return jax.shard_map(per_device, mesh=mesh, in_specs=placed, out_specs=P("seq", "mp"), check_vma=False)
```

profile of v0, /device:TPU:2, one launch (start us, length us, event | category | flops | bytes accessed | tf_op | source)
XLA Modules:
  0.0 115.1 jit_solution(15365586539183365252)
XLA Ops:
  0.0 2.1 %shard_map.104 = (f32[3,128,128]{2,1,0:T(8,128)}, f32[3,128,128]{2,1,0:T(8,128)}, f32[3,128,128]{2,1,0:T(8,128)}, f32[3,128,128]{2,1,0:T(8,128)}) custom-call(f32[128,512]{1,0:T(8,128)} %q_ref.1, f32[128,512]{1,0:T(8,128)} %k_ref.1, f32[128,512]{1,0:T(8,128)} %v_ref.1), custom_call_target="tpu_custom_call" | custom-call | tf_op jit(solution)/shard_map/pallas_call | solution.py:328
  2.1 3.3 %collective-permute-start = (f32[3,128,128]{2,1,0:T(8,128)}, f32[3,128,128]{2,1,0:T(8,128)S(1)}, u32[]{:S(2)}, u32[]{:S(2)}) collective-permute-start(f32[3,128,128]{2,1,0:T(8,128)} %get-tuple-element.30), channel_id=1, source_target_pairs={{0,64},{8,72},{16,80},{24,88},{32,96},{40,104},{48,112},{56,120},{... | collective-permute-start | bytes 589832 | tf_op jit(solution)/shard_map/ppermute | solution.py:323
  5.4 5.4 %collective-permute-start.1 = (f32[3,128,128]{2,1,0:T(8,128)}, f32[3,128,128]{2,1,0:T(8,128)S(1)}, u32[]{:S(2)}, u32[]{:S(2)}) collective-permute-start(f32[3,128,128]{2,1,0:T(8,128)} %get-tuple-element.31), channel_id=1, source_target_pairs={{0,128},{8,136},{16,144},{24,152},{32,160},{40,168},{48,176},{56,1... | collective-permute-start | bytes 589832 | tf_op jit(solution)/shard_map/ppermute | solution.py:323
  10.8 2.7 %collective-permute-start.2 = (f32[3,128,128]{2,1,0:T(8,128)}, f32[3,128,128]{2,1,0:T(8,128)S(1)}, u32[]{:S(2)}, u32[]{:S(2)}) collective-permute-start(f32[3,128,128]{2,1,0:T(8,128)} %get-tuple-element.32), channel_id=1, source_target_pairs={{0,192},{8,200},{16,208},{24,216},{32,224},{40,232},{48,240},{56,2... | collective-permute-start | bytes 589832 | tf_op jit(solution)/shard_map/ppermute | solution.py:323
  13.4 3.2 %shard_map.100 = (f32[96,8,128]{2,1,0:T(8,128)}, f32[128,512]{1,0:T(8,128)}, f32[128,512]{1,0:T(8,128)}, f32[2,8,512]{2,1,0:T(8,128)}, f32[3,7,512]{2,1,0:T(8,128)}) custom-call(s32[32]{0:T(128)} %place_ref.9, s32[32,128]{1,0:T(8,128)} %bitcast.11, f32[3,128,512]{2,1,0:T(8,128)} %bitcast.9, f32[3,7,32]{2,1,0:T(8,128)} %bitcast.16), custom_call_target="tpu_custom_call" | custom-call | tf_op jit(solution)/shard_map/pallas_call | solution.py:333
  16.7 4.2 %all-to-all-start = ((f32[32,24,128]{2,1,0:T(8,128)}), f32[32,24,128]{2,1,0:T(8,128)S(1)}, u32[]{:S(2)}, u32[]{:S(2)}) async-start(f32[32,24,128]{2,1,0:T(8,128)} %bitcast.10), calls=%async_computation | async-start | bytes 786432 | tf_op jit(solution)/shard_map/all_to_all | solution.py:339
  20.9 0.0 collective-permute-done.a1
  21.0 1.8 %collective-permute-done.1.a2 = f32[3,128,128]{2,1,0:T(8,128)S(1)} collective-permute-done((f32[3,128,128]{2,1,0:T(8,128)}, f32[3,128,128]{2,1,0:T(8,128)S(1)}, u32[]{:S(2)}, u32[]{:S(2)}) %collective-permute-start.1) | collective-permute-done | bytes 196640 | tf_op jit(solution)/shard_map/ppermute | solution.py:323
  22.8 7.9 %collective-permute-done.2.a3 = f32[3,128,128]{2,1,0:T(8,128)S(1)} collective-permute-done((f32[3,128,128]{2,1,0:T(8,128)}, f32[3,128,128]{2,1,0:T(8,128)S(1)}, u32[]{:S(2)}, u32[]{:S(2)}) %collective-permute-start.2) | collective-permute-done | bytes 196640 | tf_op jit(solution)/shard_map/ppermute | solution.py:323
  30.7 0.6 copy-done.6
  31.3 0.0 collective-permute-start.9
  31.3 0.4 collective-permute-start.5
  31.8 0.0 collective-permute-start.3
  31.8 0.3 copy-done.1
  32.1 1.5 %collective-permute-start.6 = (f32[4,128,128]{2,1,0:T(8,128)S(1)}, f32[4,128,128]{2,1,0:T(8,128)S(1)}, u32[]{:S(2)}, u32[]{:S(2)}) collective-permute-start(f32[4,128,128]{2,1,0:T(8,128)S(1)} %pad_maximum_fusion.1.rest_1_), channel_id=1, source_target_pairs={{0,16},{8,24},{16,0},{24,8},{32,48},{40,56},{48,32},{56,40},{64,80... | collective-permute-start | bytes 786440 | tf_op jit(solution)/shard_map/ppermute | solution.py:326
  33.5 5.2 %all-to-all-done.r_ref = f32[32,24,128]{2,1,0:T(8,128)S(1)} async-done(((f32[32,24,128]{2,1,0:T(8,128)}), f32[32,24,128]{2,1,0:T(8,128)S(1)}, u32[]{:S(2)}, u32[]{:S(2)}) %all-to-all-start) | async-done | bytes 393248 | tf_op jit(solution)/shard_map/all_to_all | solution.py:339
  38.7 0.8 copy-done
  39.5 1.9 %shard_map.102 = f32[32,24,128]{2,1,0:T(8,128)} custom-call(s32[32]{0:T(128)} %place_ref.9, f32[32,24,128]{2,1,0:T(8,128)} %copy-done), custom_call_target="tpu_custom_call" | custom-call | tf_op jit(solution)/shard_map/pallas_call | solution.py:355
  41.4 7.5 %all-to-all-start.1 = ((f32[32,24,128]{2,1,0:T(8,128)}), f32[32,24,128]{2,1,0:T(8,128)S(1)}, u32[]{:S(2)}, u32[]{:S(2)}) async-start(f32[32,24,128]{2,1,0:T(8,128)} %shard_map.102), calls=%async_computation.1 | async-start | bytes 786432 | tf_op jit(solution)/shard_map/all_to_all | solution.py:358
  48.8 1.6 %collective-permute-start.10 = (f32[4,128,128]{2,1,0:T(8,128)S(1)}, f32[4,128,128]{2,1,0:T(8,128)S(1)}, u32[]{:S(2)}, u32[]{:S(2)}) collective-permute-start(f32[4,128,128]{2,1,0:T(8,128)S(1)} %pad_maximum_fusion.1.rest_1_), channel_id=1, source_target_pairs={{0,32},{8,40},{16,48},{24,56},{32,0},{40,8},{48,16},{56,24},{64,96... | collective-permute-start | bytes 786440 | tf_op jit(solution)/shard_map/ppermute | solution.py:326
  50.4 0.0 collective-permute-done.9.rest_8_
  50.4 0.1 collective-permute-start.4
  50.5 0.0 collective-permute-done.5.rest_4_
  50.5 0.6 collective-permute-start.13
  51.2 0.0 collective-permute-done.3.rest_2_
  51.2 0.1 collective-permute-start.11
  51.3 0.0 collective-permute-done.6.rest_5_
  51.3 0.4 collective-permute-start.14
  51.7 14.3 %collective-permute-done.10.rest_9_ = f32[4,128,128]{2,1,0:T(8,128)S(1)} collective-permute-done((f32[4,128,128]{2,1,0:T(8,128)S(1)}, f32[4,128,128]{2,1,0:T(8,128)S(1)}, u32[]{:S(2)}, u32[]{:S(2)}) %collective-permute-start.10) | collective-permute-done | bytes 262176 | tf_op jit(solution)/shard_map/ppermute | solution.py:326
  66.0 0.0 collective-permute-start.8
  66.0 0.0 collective-permute-done.4.rest_3_
  66.0 0.5 collective-permute-start.7
  66.5 0.0 collective-permute-done.13.rest_12_
  66.5 0.1 collective-permute-start.12
  66.6 0.0 collective-permute-done.11.rest_10_
  66.6 0.4 collective-permute-start.15
  67.0 4.0 %collective-permute-done.14.rest_13_ = f32[4,128,128]{2,1,0:T(8,128)S(1)} collective-permute-done((f32[4,128,128]{2,1,0:T(8,128)S(1)}, f32[4,128,128]{2,1,0:T(8,128)S(1)}, u32[]{:S(2)}, u32[]{:S(2)}) %collective-permute-start.14) | collective-permute-done | bytes 262176 | tf_op jit(solution)/shard_map/ppermute | solution.py:326
  71.0 0.0 collective-permute-start.16
  71.0 0.0 collective-permute-done.7.rest_6_
  71.0 0.0 collective-permute-done.12.rest_11_
  71.1 0.0 collective-permute-done.8.rest_7_
  71.1 0.0 collective-permute-done.15.rest_14_
  71.1 0.7 copy-done.18
  71.8 0.7 copy-done.19
  72.5 0.1 collective-permute-done.16.rest_15_
  72.8 7.1 %shard_map.105 = (f32[128,128]{1,0:T(8,128)}, f32[128,128]{1,0:T(8,128)}, f32[128,128]{1,0:T(8,128)}, f32[128,128]{1,0:T(8,128)}) custom-call(s32[32]{0:T(128)} %place_ref.9, s32[32,128]{1,0:T(8,128)} %bitcast.12, f32[3,128,128]{2,1,0:T(8,128)} %get-tuple-element.29.a0, f32[3,128,128]{2,1,0:T(8,128)} %copy-done.4, f32[3,128,128]{2,1,0:T(8,128)} %copy-done.5, ...), custom_call_target="tpu_custom_call" | custom-call | tf_op jit(solution)/shard_map/pallas_call | solution.py:363
  79.8 2.8 %collective-permute-start.17 = (f32[128,128]{1,0:T(8,128)}, f32[128,128]{1,0:T(8,128)S(1)}, u32[]{:S(2)}, u32[]{:S(2)}) collective-permute-start(f32[128,128]{1,0:T(8,128)} %get-tuple-element.34), channel_id=1, source_target_pairs={{0,192},{8,200},{16,208},{24,216},{32,224},{40,232},{48,240},{56,2... | collective-permute-start | bytes 196616 | tf_op jit(solution)/shard_map/ppermute | solution.py:323
  82.6 3.3 %collective-permute-start.18 = (f32[128,128]{1,0:T(8,128)}, f32[128,128]{1,0:T(8,128)S(1)}, u32[]{:S(2)}, u32[]{:S(2)}) collective-permute-start(f32[128,128]{1,0:T(8,128)} %get-tuple-element.35), channel_id=1, source_target_pairs={{0,128},{8,136},{16,144},{24,152},{32,160},{40,168},{48,176},{56,1... | collective-permute-start | bytes 196616 | tf_op jit(solution)/shard_map/ppermute | solution.py:323
  85.9 1.5 %collective-permute-start.19 = (f32[128,128]{1,0:T(8,128)}, f32[128,128]{1,0:T(8,128)S(1)}, u32[]{:S(2)}, u32[]{:S(2)}) collective-permute-start(f32[128,128]{1,0:T(8,128)} %get-tuple-element.36), channel_id=1, source_target_pairs={{0,64},{8,72},{16,80},{24,88},{32,96},{40,104},{48,112},{56,120},{... | collective-permute-start | bytes 196616 | tf_op jit(solution)/shard_map/ppermute | solution.py:323
  87.4 4.9 %shard_map.101 = (f32[128,512]{1,0:T(8,128)}, f32[128,512]{1,0:T(8,128)}) custom-call(s32[32]{0:T(128)} %place_ref.9, s32[32,128]{1,0:T(8,128)} %bitcast.13, f32[32,128]{1,0:T(8,128)} %bitcast.15, f32[1,32]{1,0:T(1,128)} %bitcast.18, f32[128,512]{1,0:T(8,128)} %get-tuple-element.23.g_ref), custom_call_target="tpu_custom_call" | custom-call | tf_op jit(solution)/shard_map/pallas_call | solution.py:342
  92.2 5.0 %shard_map.103.hy_ref = f32[128,512]{1,0:T(8,128)} custom-call(s32[32]{0:T(128)} %place_ref.9, s32[32,128]{1,0:T(8,128)} %bitcast.14, f32[3,7,512]{2,1,0:T(8,128)} %get-tuple-element.22.short_ref, f32[128,512]{1,0:T(8,128)} %get-tuple-element.24.t_ref, f32[128,512]{1,0:T(8,128)} %get-tuple-element.25.f0_ref, f32[128,512]{1,0:T(8,128)} %get-tuple-element.26.own_ref, ...), custom_call_target="tpu_custom_call" | custom-call | tf_op jit(solution)/shard_map/pallas_call | solution.py:381
  97.2 0.0 collective-permute-done.17.a1
  97.2 0.0 collective-permute-done.18.a2
  97.3 1.9 %shard_map.106 = (f32[128,512]{1,0:T(8,128)}, f32[8,128]{1,0:T(8,128)}) custom-call(f32[128,512]{1,0:T(8,128)} %shard_map.103.hy_ref, f32[128,128]{1,0:T(8,128)} %get-tuple-element.33.a0, f32[128,128]{1,0:T(8,128)S(1)} %collective-permute-done.17.a1, f32[128,128]{1,0:T(8,128)S(1)} %collective-permute-done.18.a2, f32[128,128]{1,0:T(8,128)S(1)} %collective-permute-done.19.a3), custom_call_target="tpu_custom_call" | custom-call | tf_op jit(solution)/shard_map/pallas_call | solution.py:384
  99.2 3.0 %collective-permute-start.22 = (f32[8,128]{1,0:T(8,128)}, f32[8,128]{1,0:T(8,128)S(1)}, u32[]{:S(2)}, u32[]{:S(2)}) collective-permute-start(f32[8,128]{1,0:T(8,128)} %get-tuple-element.38), channel_id=1, source_target_pairs={{0,6},{1,7},{2,0},{3,1},{4,2},{5,3},{6,4},{7,5},{8,14},{9,15},{10,... | collective-permute-start | bytes 12296 | tf_op jit(solution)/shard_map/ppermute | solution.py:387
  102.2 0.0 collective-permute-start.21
  102.2 2.2 %collective-permute-start.20 = (f32[8,128]{1,0:T(8,128)}, f32[8,128]{1,0:T(8,128)S(1)}, u32[]{:S(2)}, u32[]{:S(2)}) collective-permute-start(f32[8,128]{1,0:T(8,128)} %get-tuple-element.38), channel_id=1, source_target_pairs={{0,4},{1,5},{2,6},{3,7},{4,0},{5,1},{6,2},{7,3},{8,12},{9,13},{10,... | collective-permute-start | bytes 12296 | tf_op jit(solution)/shard_map/ppermute | solution.py:387
  104.4 0.0 collective-permute-done.22
  104.4 2.8 %collective-permute-done.21 = f32[8,128]{1,0:T(8,128)S(1)} collective-permute-done((f32[8,128]{1,0:T(8,128)}, f32[8,128]{1,0:T(8,128)S(1)}, u32[]{:S(2)}, u32[]{:S(2)}) %collective-permute-start.21) | collective-permute-done | bytes 4128 | tf_op jit(solution)/shard_map/ppermute | solution.py:387
  107.3 0.3 collective-permute-done.20
  107.6 0.7 add_add_fusion.sq_ref
  108.2 2.1 %collective-permute-start.23 = (f32[8,128]{1,0:T(8,128)S(1)}, f32[8,128]{1,0:T(8,128)S(1)}, u32[]{:S(2)}, u32[]{:S(2)}) collective-permute-start(f32[8,128]{1,0:T(8,128)S(1)} %add_add_fusion.sq_ref), channel_id=1, source_target_pairs={{0,1},{1,0},{2,3},{3,2},{4,5},{5,4},{6,7},{7,6},{8,9},{9,8},{10,11... | collective-permute-start | bytes 12296 | tf_op jit(solution)/shard_map/ppermute | solution.py:326
  110.4 3.0 %collective-permute-done.23.other_ref = f32[8,128]{1,0:T(8,128)S(1)} collective-permute-done((f32[8,128]{1,0:T(8,128)S(1)}, f32[8,128]{1,0:T(8,128)S(1)}, u32[]{:S(2)}, u32[]{:S(2)}) %collective-permute-start.23) | collective-permute-done | bytes 4128 | tf_op jit(solution)/shard_map/ppermute | solution.py:326
  113.4 1.8 %shard_map.107 = f32[128,512]{1,0:T(8,128)} custom-call(f32[128,512]{1,0:T(8,128)} %get-tuple-element.37.y_ref, f32[8,128]{1,0:T(8,128)} %copy-done.20, f32[8,128]{1,0:T(8,128)S(1)} %collective-permute-done.23.other_ref, f32[1,512]{1,0:T(1,128)} %bitcast.17), custom_call_target="tpu_custom_call" | custom-call | tf_op jit(solution)/shard_map/pallas_call | solution.py:391
  (45 shorter events, 0.2 us)
Async XLA Ops:
  2.1 18.8 %collective-permute-start = (f32[3,128,128]{2,1,0:T(8,128)}, f32[3,128,128]{2,1,0:T(8,128)S(1)}, u32[]{:S(2)}, u32[]{:S(2)}) collective-permute-start(f32[3,128,128]{2,1,0:T(8,128)} %get-tuple-element.30), channel_id=1, source_target_pairs={{0,64},{8,72},{16,80},{24,88},{32,96},{40,104},{48,112},{56,120},{... | collective-permute-start | bytes 589832 | tf_op jit(solution)/shard_map/ppermute | solution.py:323
  5.4 17.3 %collective-permute-start.1 = (f32[3,128,128]{2,1,0:T(8,128)}, f32[3,128,128]{2,1,0:T(8,128)S(1)}, u32[]{:S(2)}, u32[]{:S(2)}) collective-permute-start(f32[3,128,128]{2,1,0:T(8,128)} %get-tuple-element.31), channel_id=1, source_target_pairs={{0,128},{8,136},{16,144},{24,152},{32,160},{40,168},{48,176},{56,1... | collective-permute-start | bytes 589832 | tf_op jit(solution)/shard_map/ppermute | solution.py:323
  10.8 19.9 %collective-permute-start.2 = (f32[3,128,128]{2,1,0:T(8,128)}, f32[3,128,128]{2,1,0:T(8,128)S(1)}, u32[]{:S(2)}, u32[]{:S(2)}) collective-permute-start(f32[3,128,128]{2,1,0:T(8,128)} %get-tuple-element.32), channel_id=1, source_target_pairs={{0,192},{8,200},{16,208},{24,216},{32,224},{40,232},{48,240},{56,2... | collective-permute-start | bytes 589832 | tf_op jit(solution)/shard_map/ppermute | solution.py:323
  16.7 4.2 %copy-start.3 = (f32[3,128,128]{2,1,0:T(8,128)S(1)}, f32[3,128,128]{2,1,0:T(8,128)}, u32[]{:S(2)}) copy-start(f32[3,128,128]{2,1,0:T(8,128)} %get-tuple-element.29.a0) | copy-start | bytes 589828
  16.7 22.0 %all-to-all-start = ((f32[32,24,128]{2,1,0:T(8,128)}), f32[32,24,128]{2,1,0:T(8,128)S(1)}, u32[]{:S(2)}, u32[]{:S(2)}) async-start(f32[32,24,128]{2,1,0:T(8,128)} %bitcast.10), calls=%async_computation | async-start | bytes 786432 | tf_op jit(solution)/shard_map/all_to_all | solution.py:339
  20.9 1.8 %copy-start.4 = (f32[3,128,128]{2,1,0:T(8,128)}, f32[3,128,128]{2,1,0:T(8,128)S(1)}, u32[]{:S(2)}) copy-start(f32[3,128,128]{2,1,0:T(8,128)S(1)} %collective-permute-done.a1) | copy-start | bytes 589828
  22.7 7.9 %copy-start.5 = (f32[3,128,128]{2,1,0:T(8,128)}, f32[3,128,128]{2,1,0:T(8,128)S(1)}, u32[]{:S(2)}) copy-start(f32[3,128,128]{2,1,0:T(8,128)S(1)} %collective-permute-done.1.a2) | copy-start | bytes 589828
  30.7 0.7 copy-start.6
  31.3 0.7 copy-start.1
  31.3 19.0 %collective-permute-start.9 = (f32[4,128,128]{2,1,0:T(8,128)S(1)}, f32[4,128,128]{2,1,0:T(8,128)S(1)}, u32[]{:S(2)}, u32[]{:S(2)}) collective-permute-start(f32[4,128,128]{2,1,0:T(8,128)S(1)} %pad_maximum_fusion.rest_0_), channel_id=1, source_target_pairs={{0,32},{8,40},{16,48},{24,56},{32,0},{40,8},{48,16},{56,24},{64,96... | collective-permute-start | bytes 786440 | tf_op jit(solution)/shard_map/ppermute | solution.py:326
  31.3 19.1 %collective-permute-start.5 = (f32[4,128,128]{2,1,0:T(8,128)S(1)}, f32[4,128,128]{2,1,0:T(8,128)S(1)}, u32[]{:S(2)}, u32[]{:S(2)}) collective-permute-start(f32[4,128,128]{2,1,0:T(8,128)S(1)} %pad_maximum_fusion.rest_0_), channel_id=1, source_target_pairs={{0,16},{8,24},{16,0},{24,8},{32,48},{40,56},{48,32},{56,40},{64,80... | collective-permute-start | bytes 786440 | tf_op jit(solution)/shard_map/ppermute | solution.py:326
  31.8 19.4 %collective-permute-start.3 = (f32[4,128,128]{2,1,0:T(8,128)S(1)}, f32[4,128,128]{2,1,0:T(8,128)S(1)}, u32[]{:S(2)}, u32[]{:S(2)}) collective-permute-start(f32[4,128,128]{2,1,0:T(8,128)S(1)} %pad_maximum_fusion.rest_0_), channel_id=1, source_target_pairs={{0,8},{8,0},{16,24},{24,16},{32,40},{40,32},{48,56},{56,48},{64,72... | collective-permute-start | bytes 786440 | tf_op jit(solution)/shard_map/ppermute | solution.py:326
  32.0 18.3 %copy-start.2 = (f32[4,128,128]{2,1,0:T(8,128)}, f32[4,128,128]{2,1,0:T(8,128)S(1)}, u32[]{:S(2)}) copy-start(f32[4,128,128]{2,1,0:T(8,128)S(1)} %pad_maximum_fusion.1.rest_1_) | copy-start | bytes 786436
  32.1 19.2 %collective-permute-start.6 = (f32[4,128,128]{2,1,0:T(8,128)S(1)}, f32[4,128,128]{2,1,0:T(8,128)S(1)}, u32[]{:S(2)}, u32[]{:S(2)}) collective-permute-start(f32[4,128,128]{2,1,0:T(8,128)S(1)} %pad_maximum_fusion.1.rest_1_), channel_id=1, source_target_pairs={{0,16},{8,24},{16,0},{24,8},{32,48},{40,56},{48,32},{56,40},{64,80... | collective-permute-start | bytes 786440 | tf_op jit(solution)/shard_map/ppermute | solution.py:326
  38.7 0.8 copy-start
  41.4 50.9 %all-to-all-start.1 = ((f32[32,24,128]{2,1,0:T(8,128)}), f32[32,24,128]{2,1,0:T(8,128)S(1)}, u32[]{:S(2)}, u32[]{:S(2)}) async-start(f32[32,24,128]{2,1,0:T(8,128)} %shard_map.102), calls=%async_computation.1 | async-start | bytes 786432 | tf_op jit(solution)/shard_map/all_to_all | solution.py:358
  48.8 17.1 %collective-permute-start.10 = (f32[4,128,128]{2,1,0:T(8,128)S(1)}, f32[4,128,128]{2,1,0:T(8,128)S(1)}, u32[]{:S(2)}, u32[]{:S(2)}) collective-permute-start(f32[4,128,128]{2,1,0:T(8,128)S(1)} %pad_maximum_fusion.1.rest_1_), channel_id=1, source_target_pairs={{0,32},{8,40},{16,48},{24,56},{32,0},{40,8},{48,16},{56,24},{64,96... | collective-permute-start | bytes 786440 | tf_op jit(solution)/shard_map/ppermute | solution.py:326
  50.4 22.3 %copy-start.7 = (f32[4,128,128]{2,1,0:T(8,128)}, f32[4,128,128]{2,1,0:T(8,128)S(1)}, u32[]{:S(2)}) copy-start(f32[4,128,128]{2,1,0:T(8,128)S(1)} %collective-permute-done.9.rest_8_) | copy-start | bytes 786436
  50.4 15.6 %collective-permute-start.4 = (f32[4,128,128]{2,1,0:T(8,128)S(1)}, f32[4,128,128]{2,1,0:T(8,128)S(1)}, u32[]{:S(2)}, u32[]{:S(2)}) collective-permute-start(f32[4,128,128]{2,1,0:T(8,128)S(1)} %pad_maximum_fusion.1.rest_1_), channel_id=1, source_target_pairs={{0,8},{8,0},{16,24},{24,16},{32,40},{40,32},{48,56},{56,48},{64,72... | collective-permute-start | bytes 786440 | tf_op jit(solution)/shard_map/ppermute | solution.py:326
  50.5 22.2 %copy-start.8 = (f32[4,128,128]{2,1,0:T(8,128)}, f32[4,128,128]{2,1,0:T(8,128)S(1)}, u32[]{:S(2)}) copy-start(f32[4,128,128]{2,1,0:T(8,128)S(1)} %collective-permute-done.5.rest_4_) | copy-start | bytes 786436
  50.5 16.0 %collective-permute-start.13 = (f32[4,128,128]{2,1,0:T(8,128)S(1)}, f32[4,128,128]{2,1,0:T(8,128)S(1)}, u32[]{:S(2)}, u32[]{:S(2)}) collective-permute-start(f32[4,128,128]{2,1,0:T(8,128)S(1)} %collective-permute-done.9.rest_8_), channel_id=1, source_target_pairs={{0,16},{8,24},{16,0},{24,8},{32,48},{40,56},{48,32},{56,40},{64,80... | collective-permute-start | bytes 786440 | tf_op jit(solution)/shard_map/ppermute | solution.py:326
  51.2 21.5 %copy-start.9 = (f32[4,128,128]{2,1,0:T(8,128)}, f32[4,128,128]{2,1,0:T(8,128)S(1)}, u32[]{:S(2)}) copy-start(f32[4,128,128]{2,1,0:T(8,128)S(1)} %collective-permute-done.3.rest_2_) | copy-start | bytes 786436
  51.2 15.4 %collective-permute-start.11 = (f32[4,128,128]{2,1,0:T(8,128)S(1)}, f32[4,128,128]{2,1,0:T(8,128)S(1)}, u32[]{:S(2)}, u32[]{:S(2)}) collective-permute-start(f32[4,128,128]{2,1,0:T(8,128)S(1)} %collective-permute-done.9.rest_8_), channel_id=1, source_target_pairs={{0,8},{8,0},{16,24},{24,16},{32,40},{40,32},{48,56},{56,48},{64,72... | collective-permute-start | bytes 786440 | tf_op jit(solution)/shard_map/ppermute | solution.py:326
  51.3 21.4 %copy-start.10 = (f32[4,128,128]{2,1,0:T(8,128)}, f32[4,128,128]{2,1,0:T(8,128)S(1)}, u32[]{:S(2)}) copy-start(f32[4,128,128]{2,1,0:T(8,128)S(1)} %collective-permute-done.6.rest_5_) | copy-start | bytes 786436
  51.3 19.7 %collective-permute-start.14 = (f32[4,128,128]{2,1,0:T(8,128)S(1)}, f32[4,128,128]{2,1,0:T(8,128)S(1)}, u32[]{:S(2)}, u32[]{:S(2)}) collective-permute-start(f32[4,128,128]{2,1,0:T(8,128)S(1)} %collective-permute-done.6.rest_5_), channel_id=1, source_target_pairs={{0,32},{8,40},{16,48},{24,56},{32,0},{40,8},{48,16},{56,24},{64,96... | collective-permute-start | bytes 786440 | tf_op jit(solution)/shard_map/ppermute | solution.py:326
  66.0 6.7 %copy-start.11 = (f32[4,128,128]{2,1,0:T(8,128)}, f32[4,128,128]{2,1,0:T(8,128)S(1)}, u32[]{:S(2)}) copy-start(f32[4,128,128]{2,1,0:T(8,128)S(1)} %collective-permute-done.10.rest_9_) | copy-start | bytes 786436
  66.0 5.1 %collective-permute-start.8 = (f32[4,128,128]{2,1,0:T(8,128)S(1)}, f32[4,128,128]{2,1,0:T(8,128)S(1)}, u32[]{:S(2)}, u32[]{:S(2)}) collective-permute-start(f32[4,128,128]{2,1,0:T(8,128)S(1)} %collective-permute-done.6.rest_5_), channel_id=1, source_target_pairs={{0,8},{8,0},{16,24},{24,16},{32,40},{40,32},{48,56},{56,48},{64,72... | collective-permute-start | bytes 786440 | tf_op jit(solution)/shard_map/ppermute | solution.py:326
  66.0 6.7 %copy-start.12 = (f32[4,128,128]{2,1,0:T(8,128)}, f32[4,128,128]{2,1,0:T(8,128)S(1)}, u32[]{:S(2)}) copy-start(f32[4,128,128]{2,1,0:T(8,128)S(1)} %collective-permute-done.4.rest_3_) | copy-start | bytes 786436
  66.0 5.0 %collective-permute-start.7 = (f32[4,128,128]{2,1,0:T(8,128)S(1)}, f32[4,128,128]{2,1,0:T(8,128)S(1)}, u32[]{:S(2)}, u32[]{:S(2)}) collective-permute-start(f32[4,128,128]{2,1,0:T(8,128)S(1)} %collective-permute-done.5.rest_4_), channel_id=1, source_target_pairs={{0,8},{8,0},{16,24},{24,16},{32,40},{40,32},{48,56},{56,48},{64,72... | collective-permute-start | bytes 786440 | tf_op jit(solution)/shard_map/ppermute | solution.py:326
  66.5 6.2 %copy-start.13 = (f32[4,128,128]{2,1,0:T(8,128)}, f32[4,128,128]{2,1,0:T(8,128)S(1)}, u32[]{:S(2)}) copy-start(f32[4,128,128]{2,1,0:T(8,128)S(1)} %collective-permute-done.13.rest_12_) | copy-start | bytes 786436
  66.5 4.5 %collective-permute-start.12 = (f32[4,128,128]{2,1,0:T(8,128)S(1)}, f32[4,128,128]{2,1,0:T(8,128)S(1)}, u32[]{:S(2)}, u32[]{:S(2)}) collective-permute-start(f32[4,128,128]{2,1,0:T(8,128)S(1)} %collective-permute-done.10.rest_9_), channel_id=1, source_target_pairs={{0,8},{8,0},{16,24},{24,16},{32,40},{40,32},{48,56},{56,48},{64,72... | collective-permute-start | bytes 786440 | tf_op jit(solution)/shard_map/ppermute | solution.py:326
  66.6 6.1 %copy-start.14 = (f32[4,128,128]{2,1,0:T(8,128)}, f32[4,128,128]{2,1,0:T(8,128)S(1)}, u32[]{:S(2)}) copy-start(f32[4,128,128]{2,1,0:T(8,128)S(1)} %collective-permute-done.11.rest_10_) | copy-start | bytes 786436
  66.6 4.5 %collective-permute-start.15 = (f32[4,128,128]{2,1,0:T(8,128)S(1)}, f32[4,128,128]{2,1,0:T(8,128)S(1)}, u32[]{:S(2)}, u32[]{:S(2)}) collective-permute-start(f32[4,128,128]{2,1,0:T(8,128)S(1)} %collective-permute-done.13.rest_12_), channel_id=1, source_target_pairs={{0,8},{8,0},{16,24},{24,16},{32,40},{40,32},{48,56},{56,48},{64,72... | collective-permute-start | bytes 786440 | tf_op jit(solution)/shard_map/ppermute | solution.py:326
  71.0 1.7 %copy-start.15 = (f32[4,128,128]{2,1,0:T(8,128)}, f32[4,128,128]{2,1,0:T(8,128)S(1)}, u32[]{:S(2)}) copy-start(f32[4,128,128]{2,1,0:T(8,128)S(1)} %collective-permute-done.14.rest_13_) | copy-start | bytes 786436
  71.0 1.7 %collective-permute-start.16 = (f32[4,128,128]{2,1,0:T(8,128)S(1)}, f32[4,128,128]{2,1,0:T(8,128)}, u32[]{:S(2)}, u32[]{:S(2)}) collective-permute-start(f32[4,128,128]{2,1,0:T(8,128)S(1)} %collective-permute-done.14.rest_13_), channel_id=1, source_target_pairs={{0,8},{8,0},{16,24},{24,16},{32,40},{40,32},{48,56},{56,48},{64,72... | collective-permute-start | bytes 786440 | tf_op jit(solution)/shard_map/ppermute | solution.py:326
  71.0 1.7 %copy-start.17 = (f32[4,128,128]{2,1,0:T(8,128)}, f32[4,128,128]{2,1,0:T(8,128)S(1)}, u32[]{:S(2)}) copy-start(f32[4,128,128]{2,1,0:T(8,128)S(1)} %collective-permute-done.7.rest_6_) | copy-start | bytes 786436
  71.0 0.8 copy-start.18
  71.1 1.7 %copy-start.16 = (f32[4,128,128]{2,1,0:T(8,128)}, f32[4,128,128]{2,1,0:T(8,128)S(1)}, u32[]{:S(2)}) copy-start(f32[4,128,128]{2,1,0:T(8,128)S(1)} %collective-permute-done.8.rest_7_) | copy-start | bytes 786436
  71.8 0.7 copy-start.19
  79.8 17.4 %collective-permute-start.17 = (f32[128,128]{1,0:T(8,128)}, f32[128,128]{1,0:T(8,128)S(1)}, u32[]{:S(2)}, u32[]{:S(2)}) collective-permute-start(f32[128,128]{1,0:T(8,128)} %get-tuple-element.34), channel_id=1, source_target_pairs={{0,192},{8,200},{16,208},{24,216},{32,224},{40,232},{48,240},{56,2... | collective-permute-start | bytes 196616 | tf_op jit(solution)/shard_map/ppermute | solution.py:323
  82.6 14.7 %collective-permute-start.18 = (f32[128,128]{1,0:T(8,128)}, f32[128,128]{1,0:T(8,128)S(1)}, u32[]{:S(2)}, u32[]{:S(2)}) collective-permute-start(f32[128,128]{1,0:T(8,128)} %get-tuple-element.35), channel_id=1, source_target_pairs={{0,128},{8,136},{16,144},{24,152},{32,160},{40,168},{48,176},{56,1... | collective-permute-start | bytes 196616 | tf_op jit(solution)/shard_map/ppermute | solution.py:323
  85.9 11.4 %collective-permute-start.19 = (f32[128,128]{1,0:T(8,128)}, f32[128,128]{1,0:T(8,128)S(1)}, u32[]{:S(2)}, u32[]{:S(2)}) collective-permute-start(f32[128,128]{1,0:T(8,128)} %get-tuple-element.36), channel_id=1, source_target_pairs={{0,64},{8,72},{16,80},{24,88},{32,96},{40,104},{48,112},{56,120},{... | collective-permute-start | bytes 196616 | tf_op jit(solution)/shard_map/ppermute | solution.py:323
  99.2 5.2 %collective-permute-start.22 = (f32[8,128]{1,0:T(8,128)}, f32[8,128]{1,0:T(8,128)S(1)}, u32[]{:S(2)}, u32[]{:S(2)}) collective-permute-start(f32[8,128]{1,0:T(8,128)} %get-tuple-element.38), channel_id=1, source_target_pairs={{0,6},{1,7},{2,0},{3,1},{4,2},{5,3},{6,4},{7,5},{8,14},{9,15},{10,... | collective-permute-start | bytes 12296 | tf_op jit(solution)/shard_map/ppermute | solution.py:387
  102.2 5.0 %collective-permute-start.21 = (f32[8,128]{1,0:T(8,128)}, f32[8,128]{1,0:T(8,128)S(1)}, u32[]{:S(2)}, u32[]{:S(2)}) collective-permute-start(f32[8,128]{1,0:T(8,128)} %get-tuple-element.38), channel_id=1, source_target_pairs={{0,2},{1,3},{2,4},{3,5},{4,6},{5,7},{6,0},{7,1},{8,10},{9,11},{10,... | collective-permute-start | bytes 12296 | tf_op jit(solution)/shard_map/ppermute | solution.py:387
  102.2 5.3 %collective-permute-start.20 = (f32[8,128]{1,0:T(8,128)}, f32[8,128]{1,0:T(8,128)S(1)}, u32[]{:S(2)}, u32[]{:S(2)}) collective-permute-start(f32[8,128]{1,0:T(8,128)} %get-tuple-element.38), channel_id=1, source_target_pairs={{0,4},{1,5},{2,6},{3,7},{4,0},{5,1},{6,2},{7,3},{8,12},{9,13},{10,... | collective-permute-start | bytes 12296 | tf_op jit(solution)/shard_map/ppermute | solution.py:387
  108.2 5.1 %copy-start.20 = (f32[8,128]{1,0:T(8,128)}, f32[8,128]{1,0:T(8,128)S(1)}, u32[]{:S(2)}) copy-start(f32[8,128]{1,0:T(8,128)S(1)} %add_add_fusion.sq_ref) | copy-start | bytes 12292
  108.2 5.1 %collective-permute-start.23 = (f32[8,128]{1,0:T(8,128)S(1)}, f32[8,128]{1,0:T(8,128)S(1)}, u32[]{:S(2)}, u32[]{:S(2)}) collective-permute-start(f32[8,128]{1,0:T(8,128)S(1)} %add_add_fusion.sq_ref), channel_id=1, source_target_pairs={{0,1},{1,0},{2,3},{3,2},{4,5},{5,4},{6,7},{7,6},{8,9},{9,8},{10,11... | collective-permute-start | bytes 12296 | tf_op jit(solution)/shard_map/ppermute | solution.py:326
where the time goes:
time: 116 us; the launch traced here: 115 us
  starting transfers between devices  43.5 us (38%)
  waiting for transfers between devices  39.5 us (34%)
  Pallas kernels  27.9 us (24%)
  local copies, waits for them, and re-layouts  3.19 us (3%)
    ppermute x15, waiting for transfers between devices, swap(): lax.ppermute(x, axis, [(b, b ^ bit) for b in range(N if axis == 'seq' els...  21.5 us
    ppermute x6, starting transfers between devices, ring(): return lax.ppermute(x, 'seq', [(b, (b + 8 * k) % N) for b in range(N)])  18.8 us
    ppermute x6, waiting for transfers between devices, ring(): return lax.ppermute(x, 'seq', [(b, (b + 8 * k) % N) for b in range(N)])  9.68 us
    ppermute x15, starting transfers between devices, swap(): lax.ppermute(x, axis, [(b, b ^ bit) for b in range(N if axis == 'seq' els...  7.8 us
    all_to_all x1, starting transfers between devices, per_device(): back = lax.all_to_all(chosen, 'seq', 0, 0, tiled=True).reshape(96, 8, 128)  7.45 us
    pallas_call x1, Pallas kernels, per_device(): call(attend_kernel, [(T, HD)] * 4, [SMEM, VMEM] + [ANY] * 20, [pltpu.VMEM...  7.06 us
    ppermute x3, starting transfers between devices, along_y(): return lax.ppermute(squares, 'mp', [(m, (m + 2 * k) % 8) for m in range(8)])  5.23 us
    all_to_all x1, waiting for transfers between devices, per_device(): pieces = lax.all_to_all(tiles.reshape(N, 24, 128), 'seq', 0, 0, tiled=True)  5.22 us
  transfers between devices with their start and end apart: 26, of which 9 were waited for; matrix products, arithmetic and copies ran while one was open for 0% of the time, Pallas kernels for 19%

commit v1 on v0

--- a/solution.py
+++ b/solution.py
@@ -221,19 +221,15 @@
     return high, (x - high.astype(F32)).astype(jnp.bfloat16)
 
 
-def dot3(a, high, low, dims):
-    def dot(x, y):
-        return lax.dot_general(x, y, (dims, ((), ())), preferred_element_type=F32)
-
-    both = dot(a, high)
-    return both[:T] + (both[T:] + dot(a[:T], low))
+def dot(a, b, dims):
+    return lax.dot_general(a, b, (dims, ((), ())), preferred_element_type=F32)
 
 
 def attend_kernel(
     place_ref, doc_ref, a0, a1, a2, a3, *rest
 ):
-    kv, rest = rest[:16], rest[16:]
-    outs, (q_ref, kv_ref, sem, kh, kl, vh, vl, s_ref, qs_ref, p_ref) = rest[:4], rest[4:]
+    kv, late, rest = rest[:14], rest[14:16], rest[16:]
+    outs, (q_ref, kv_ref, sem, k_ref, v_ref, s_ref, qs_ref, p_ref) = rest[:4], rest[4:]
     copies = []
 
     def fetch(src, dst):
@@ -249,39 +245,50 @@
     g = lax.rem(me, 8)
 
     for x in range(8):
-        copies[2 * x].wait()
-        copies[2 * x + 1].wait()
+        if x < 7:
+            copies[2 * x].wait()
+            copies[2 * x + 1].wait()
         for k in range(4):
             at = place_ref[lax.rem(zq + 4 - k, 4) * 8 + lax.bitwise_xor(g, x)]
             rows = pl.ds(pl.multiple_of(at * T, T), T)
-            kh[rows, :], kl[rows, :] = split(kv_ref[x, 0, k])
-            vh[rows, :], vl[rows, :] = split(kv_ref[x, 1, k])
-    for copy in copies[16:]:
+            k_ref[rows, :HD], k_ref[rows, HD:] = split(kv_ref[x, 0, k] if x < 7 else late[0][k])
+            v_ref[rows, :HD], v_ref[rows, HD:] = split(kv_ref[x, 1, k] if x < 7 else late[1][k])
+    for copy in copies[14:]:
         copy.wait()
     scale = 1.0 / jnp.sqrt(jnp.float32(HD))
     ahead = iota((T, T), 1) - iota((T, T), 0)
+    home = [place_ref[lax.rem(zq + 4 - i, 4) * 8 + g] for i in range(4)]
+    first = [jnp.maximum(c - (NB - 1), 0) for c in home]
+    window = [pl.ds(pl.multiple_of(f * T, T), NB * T) for f in first]
+
+    def score(i):
+        high, low = split(q_ref[i])
+        qs_ref[i, :T, :HD], qs_ref[i, :T, HD:] = high, high
+        qs_ref[i, T:, :HD], qs_ref[i, T:, HD:] = low, jnp.zeros_like(low)
+        both = dot(qs_ref[i], k_ref[window[i], :], ((1,), (1,)))
+        s_ref[i % 2] = (both[:T] + both[T:]) * scale
+
+    score(0)
     for i in range(4):
-        c = place_ref[lax.rem(zq + 4 - i, 4) * 8 + g]
-        first = jnp.maximum(c - (NB - 1), 0)
-        col = column(doc_row(doc_ref, c))
-        qs_ref[:T, :], qs_ref[T:, :] = split(q_ref[i])
-        rows = pl.ds(pl.multiple_of(first * T, T), NB * T)
-        s_ref[...] = dot3(qs_ref[...], kh[rows, :], kl[rows, :], ((1,), (1,))) * scale
+        if i < 3:
+            score(i + 1)
+        col = column(doc_row(doc_ref, home[i]))
         top = None
         for n in range(NB):
             cols = slice(n * T, n * T + T)
-            allowed = (doc_row(doc_ref, first + n) == col) & (ahead <= (c - first - n) * T)
-            s = jnp.where(allowed, s_ref[:, cols], -1e30)
-            s_ref[:, cols] = s
+            allowed = (doc_row(doc_ref, first[i] + n) == col) & (ahead <= (home[i] - first[i] - n) * T)
+            s = jnp.where(allowed, s_ref[i % 2, :, cols], -1e30)
+            s_ref[i % 2, :, cols] = s
             top = s if top is None else jnp.maximum(top, s)
         top = jnp.max(top, axis=1, keepdims=True)
         total = jnp.zeros((T, T), F32)
         for n in range(NB):
             cols = slice(n * T, n * T + T)
-            p = jnp.exp(s_ref[:, cols] - top)
+            p = jnp.exp(s_ref[i % 2, :, cols] - top)
             total = total + p
-            p_ref[:T, cols], p_ref[T:, cols] = split(p)
-        acc = dot3(p_ref[...], vh[rows, :], vl[rows, :], ((1,), (0,)))
+            p_ref[i % 2, :T, cols], p_ref[i % 2, T:, cols] = split(p)
+        acc = dot(p_ref[i % 2], v_ref[window[i], :], ((1,), (0,)))
+        acc = acc[:T, :HD] + (acc[:T, HD:] + acc[T:, :HD])
         outs[i][...] = acc / jnp.sum(total, axis=1, keepdims=True)
 
 
@@ -348,9 +355,10 @@
     xk = swap(k0, "seq", 2)
     dk = swap(zk, "seq", 2)
     dv = swap(xv, "seq", 4)
-    ck, cv, cxk, cxv, czk, czv, cdk, cdv = (
-        swap(a, "seq", 1) for a in (k0, v0, xk, xv, zk, zv, dk, dv)
-    )
+    ck, cv = swap(k0, "seq", 1), swap(v0, "seq", 1)
+    czk, cxv = swap(zk, "seq", 1), swap(xv, "seq", 1)
+    czv, cxk = swap(zv, "seq", 1), swap(xk, "seq", 1)
+    cdk, cdv = swap(dk, "seq", 1), swap(dv, "seq", 1)
 
     chosen = call(select_kernel, [(N, 24, 128)], [SMEM, VMEM], [pltpu.SMEM((N,), jnp.int32)])(
         placement_list, hbm(pieces)
@@ -359,19 +367,20 @@
 
     bf = jnp.bfloat16
     pieces_kv = (k0, v0, ck, cv, xk, xv, cxk, cxv, zk, zv, czk, czv, dk, dv, cdk, cdv)
-    near = [hbm(a) for a in (*held[1:], *pieces_kv)]
+    near = [hbm(a) for a in (*held[1:], *pieces_kv[:14])]
+    near += [vmem(cdk), vmem(cdv)]
     attended = call(
         attend_kernel,
         [(T, HD)] * 4,
-        [SMEM, VMEM] + [ANY] * 20,
+        [SMEM, VMEM] + [ANY] * 18 + [VMEM] * 2,
         [
             pltpu.VMEM((4, T, HD), F32),
-            pltpu.VMEM((8, 2, 4, T, HD), F32),
-            pltpu.SemaphoreType.DMA((20,)),
-            *[pltpu.VMEM((N * T, HD), bf)] * 4,
-            pltpu.VMEM((T, NB * T), F32),
-            pltpu.VMEM((2 * T, HD), bf),
-            pltpu.VMEM((2 * T, NB * T), bf),
+            pltpu.VMEM((7, 2, 4, T, HD), F32),
+            pltpu.SemaphoreType.DMA((18,)),
+            *[pltpu.VMEM((N * T, 2 * HD), bf)] * 2,
+            pltpu.VMEM((2, T, NB * T), F32),
+            pltpu.VMEM((4, 2 * T, 2 * HD), bf),
+            pltpu.VMEM((2, 2 * T, NB * T), bf),
         ],
     )(placement_list, docs, held[0], *near)
     home = [attended[0]] + [None] * 3

time: 116 us -> 115 us (level)
    unnamed x42 -> x40, local copies, waits for them, and re-layouts: 3.15 us -> 2.56 us
  transfers between devices with their start and end apart: 26 -> 26, of which waited for: 9 -> 9; matrix products, arithmetic and copies ran while one was open for 0% -> 0% of each run, Pallas kernels for 19% -> 18%
where the time goes in v1:
time: 115 us; the launch traced here: 114 us
  starting transfers between devices  43.5 us (38%)
  waiting for transfers between devices  39.9 us (35%)
  Pallas kernels  26.8 us (23%)
  local copies, waits for them, and re-layouts  2.6 us (2%)
    ppermute x15, waiting for transfers between devices, swap(): lax.ppermute(x, axis, [(b, b ^ bit) for b in range(N if axis == 'seq' els...  21.9 us
    ppermute x6, starting transfers between devices, ring(): return lax.ppermute(x, 'seq', [(b, (b + 8 * k) % N) for b in range(N)])  18.8 us
    ppermute x6, waiting for transfers between devices, ring(): return lax.ppermute(x, 'seq', [(b, (b + 8 * k) % N) for b in range(N)])  9.67 us
    ppermute x15, starting transfers between devices, swap(): lax.ppermute(x, axis, [(b, b ^ bit) for b in range(N if axis == 'seq' els...  7.81 us
    all_to_all x1, starting transfers between devices, per_device(): back = lax.all_to_all(chosen, 'seq', 0, 0, tiled=True).reshape(96, 8, 128)  7.45 us
    pallas_call x1, Pallas kernels, per_device(): call(attend_kernel, [(T, HD)] * 4, [SMEM, VMEM] + [ANY] * 18 + [VMEM] * 2...  5.99 us
    all_to_all x1, waiting for transfers between devices, per_device(): pieces = lax.all_to_all(tiles.reshape(N, 24, 128), 'seq', 0, 0, tiled=True)  5.22 us
    ppermute x3, starting transfers between devices, along_y(): return lax.ppermute(squares, 'mp', [(m, (m + 2 * k) % 8) for m in range(8)])  5.22 us
  transfers between devices with their start and end apart: 26, of which 9 were waited for; matrix products, arithmetic and copies ran while one was open for 0% of the time, Pallas kernels for 18%

profile of v1, /device:TPU:2, one launch (start us, length us, event | category | flops | bytes accessed | tf_op | source)
XLA Modules:
  0.0 113.9 jit_solution(1968463230534947025)
XLA Ops:
  0.0 2.1 %shard_map.104 = (f32[3,128,128]{2,1,0:T(8,128)}, f32[3,128,128]{2,1,0:T(8,128)}, f32[3,128,128]{2,1,0:T(8,128)}, f32[3,128,128]{2,1,0:T(8,128)}) custom-call(f32[128,512]{1,0:T(8,128)} %q_ref.1, f32[128,512]{1,0:T(8,128)} %k_ref.1, f32[128,512]{1,0:T(8,128)} %v_ref.1), custom_call_target="tpu_custom_call" | custom-call | tf_op jit(solution)/shard_map/pallas_call | solution.py:335
  2.1 3.3 %collective-permute-start = (f32[3,128,128]{2,1,0:T(8,128)}, f32[3,128,128]{2,1,0:T(8,128)S(1)}, u32[]{:S(2)}, u32[]{:S(2)}) collective-permute-start(f32[3,128,128]{2,1,0:T(8,128)} %get-tuple-element.30), channel_id=1, source_target_pairs={{0,64},{8,72},{16,80},{24,88},{32,96},{40,104},{48,112},{56,120},{... | collective-permute-start | bytes 589832 | tf_op jit(solution)/shard_map/ppermute | solution.py:330
  5.4 5.4 %collective-permute-start.1 = (f32[3,128,128]{2,1,0:T(8,128)}, f32[3,128,128]{2,1,0:T(8,128)S(1)}, u32[]{:S(2)}, u32[]{:S(2)}) collective-permute-start(f32[3,128,128]{2,1,0:T(8,128)} %get-tuple-element.31), channel_id=1, source_target_pairs={{0,128},{8,136},{16,144},{24,152},{32,160},{40,168},{48,176},{56,1... | collective-permute-start | bytes 589832 | tf_op jit(solution)/shard_map/ppermute | solution.py:330
  10.8 2.7 %collective-permute-start.2 = (f32[3,128,128]{2,1,0:T(8,128)}, f32[3,128,128]{2,1,0:T(8,128)S(1)}, u32[]{:S(2)}, u32[]{:S(2)}) collective-permute-start(f32[3,128,128]{2,1,0:T(8,128)} %get-tuple-element.32), channel_id=1, source_target_pairs={{0,192},{8,200},{16,208},{24,216},{32,224},{40,232},{48,240},{56,2... | collective-permute-start | bytes 589832 | tf_op jit(solution)/shard_map/ppermute | solution.py:330
  13.4 3.2 %shard_map.100 = (f32[96,8,128]{2,1,0:T(8,128)}, f32[128,512]{1,0:T(8,128)}, f32[128,512]{1,0:T(8,128)}, f32[2,8,512]{2,1,0:T(8,128)}, f32[3,7,512]{2,1,0:T(8,128)}) custom-call(s32[32]{0:T(128)} %place_ref.9, s32[32,128]{1,0:T(8,128)} %bitcast.11, f32[3,128,512]{2,1,0:T(8,128)} %bitcast.9, f32[3,7,32]{2,1,0:T(8,128)} %bitcast.16), custom_call_target="tpu_custom_call" | custom-call | tf_op jit(solution)/shard_map/pallas_call | solution.py:340
  16.7 4.2 %all-to-all-start = ((f32[32,24,128]{2,1,0:T(8,128)}), f32[32,24,128]{2,1,0:T(8,128)S(1)}, u32[]{:S(2)}, u32[]{:S(2)}) async-start(f32[32,24,128]{2,1,0:T(8,128)} %bitcast.10), calls=%async_computation | async-start | bytes 786432 | tf_op jit(solution)/shard_map/all_to_all | solution.py:346
  20.9 0.0 collective-permute-done.a1
  20.9 1.8 %collective-permute-done.1.a2 = f32[3,128,128]{2,1,0:T(8,128)S(1)} collective-permute-done((f32[3,128,128]{2,1,0:T(8,128)}, f32[3,128,128]{2,1,0:T(8,128)S(1)}, u32[]{:S(2)}, u32[]{:S(2)}) %collective-permute-start.1) | collective-permute-done | bytes 196640 | tf_op jit(solution)/shard_map/ppermute | solution.py:330
  22.7 7.9 %collective-permute-done.2.a3 = f32[3,128,128]{2,1,0:T(8,128)S(1)} collective-permute-done((f32[3,128,128]{2,1,0:T(8,128)}, f32[3,128,128]{2,1,0:T(8,128)S(1)}, u32[]{:S(2)}, u32[]{:S(2)}) %collective-permute-start.2) | collective-permute-done | bytes 196640 | tf_op jit(solution)/shard_map/ppermute | solution.py:330
  30.7 0.6 copy-done.6
  31.3 0.0 collective-permute-start.9
  31.3 0.4 collective-permute-start.5
  31.7 0.0 collective-permute-start.3
  31.8 0.3 copy-done.1
  32.0 1.4 %collective-permute-start.6 = (f32[4,128,128]{2,1,0:T(8,128)S(1)}, f32[4,128,128]{2,1,0:T(8,128)S(1)}, u32[]{:S(2)}, u32[]{:S(2)}) collective-permute-start(f32[4,128,128]{2,1,0:T(8,128)S(1)} %pad_maximum_fusion.1.rest_1_), channel_id=1, source_target_pairs={{0,16},{8,24},{16,0},{24,8},{32,48},{40,56},{48,32},{56,40},{64,80... | collective-permute-start | bytes 786440 | tf_op jit(solution)/shard_map/ppermute | solution.py:333
  33.5 5.2 %all-to-all-done.r_ref = f32[32,24,128]{2,1,0:T(8,128)S(1)} async-done(((f32[32,24,128]{2,1,0:T(8,128)}), f32[32,24,128]{2,1,0:T(8,128)S(1)}, u32[]{:S(2)}, u32[]{:S(2)}) %all-to-all-start) | async-done | bytes 393248 | tf_op jit(solution)/shard_map/all_to_all | solution.py:346
  38.7 0.8 copy-done
  39.5 1.9 %shard_map.102 = f32[32,24,128]{2,1,0:T(8,128)} custom-call(s32[32]{0:T(128)} %place_ref.9, f32[32,24,128]{2,1,0:T(8,128)} %copy-done), custom_call_target="tpu_custom_call" | custom-call | tf_op jit(solution)/shard_map/pallas_call | solution.py:363
  41.3 7.5 %all-to-all-start.1 = ((f32[32,24,128]{2,1,0:T(8,128)}), f32[32,24,128]{2,1,0:T(8,128)S(1)}, u32[]{:S(2)}, u32[]{:S(2)}) async-start(f32[32,24,128]{2,1,0:T(8,128)} %shard_map.102), calls=%async_computation.1 | async-start | bytes 786432 | tf_op jit(solution)/shard_map/all_to_all | solution.py:366
  48.8 1.6 %collective-permute-start.10 = (f32[4,128,128]{2,1,0:T(8,128)S(1)}, f32[4,128,128]{2,1,0:T(8,128)S(1)}, u32[]{:S(2)}, u32[]{:S(2)}) collective-permute-start(f32[4,128,128]{2,1,0:T(8,128)S(1)} %pad_maximum_fusion.1.rest_1_), channel_id=1, source_target_pairs={{0,32},{8,40},{16,48},{24,56},{32,0},{40,8},{48,16},{56,24},{64,96... | collective-permute-start | bytes 786440 | tf_op jit(solution)/shard_map/ppermute | solution.py:333
  50.3 0.0 collective-permute-done.9.rest_8_
  50.4 0.1 collective-permute-start.4
  50.5 0.0 collective-permute-done.5.rest_4_
  50.5 0.6 collective-permute-start.13
  51.1 0.0 collective-permute-done.3.rest_2_
  51.1 0.1 collective-permute-start.11
  51.2 0.0 collective-permute-done.6.rest_5_
  51.2 0.4 collective-permute-start.14
  51.6 14.3 %collective-permute-done.10.rest_9_ = f32[4,128,128]{2,1,0:T(8,128)S(1)} collective-permute-done((f32[4,128,128]{2,1,0:T(8,128)S(1)}, f32[4,128,128]{2,1,0:T(8,128)S(1)}, u32[]{:S(2)}, u32[]{:S(2)}) %collective-permute-start.10) | collective-permute-done | bytes 262176 | tf_op jit(solution)/shard_map/ppermute | solution.py:333
  65.9 0.0 collective-permute-start.8
  65.9 0.0 collective-permute-done.4.rest_3_
  66.0 0.5 collective-permute-start.7
  66.5 0.0 collective-permute-done.13.rest_12_
  66.5 0.1 collective-permute-start.12
  66.6 0.0 collective-permute-done.11.rest_10_
  66.6 0.4 collective-permute-start.15
  67.0 4.0 %collective-permute-done.14.rest_13_ = f32[4,128,128]{2,1,0:T(8,128)S(1)} collective-permute-done((f32[4,128,128]{2,1,0:T(8,128)S(1)}, f32[4,128,128]{2,1,0:T(8,128)S(1)}, u32[]{:S(2)}, u32[]{:S(2)}) %collective-permute-start.14) | collective-permute-done | bytes 262176 | tf_op jit(solution)/shard_map/ppermute | solution.py:333
  71.0 0.0 collective-permute-start.16
  71.0 0.0 collective-permute-done.7.rest_6_
  71.0 0.0 collective-permute-done.12.rest_11_
  71.0 0.0 collective-permute-done.8.rest_7_
  71.0 0.0 collective-permute-done.15.rest_14_
  71.1 0.7 copy-done.17
  71.7 0.1 copy-done.18
  71.8 0.1 copy-done.16
  71.9 0.6 collective-permute-done.16.rest_15_
  72.6 6.0 %shard_map.105 = (f32[128,128]{1,0:T(8,128)}, f32[128,128]{1,0:T(8,128)}, f32[128,128]{1,0:T(8,128)}, f32[128,128]{1,0:T(8,128)}) custom-call(s32[32]{0:T(128)} %place_ref.9, s32[32,128]{1,0:T(8,128)} %bitcast.12, f32[3,128,128]{2,1,0:T(8,128)} %get-tuple-element.29.a0, f32[3,128,128]{2,1,0:T(8,128)} %copy-done.4, f32[3,128,128]{2,1,0:T(8,128)} %copy-done.5, ...), custom_call_target="tpu_custom_call" | custom-call | tf_op jit(solution)/shard_map/pallas_call | solution.py:372
  78.6 2.7 %collective-permute-start.17 = (f32[128,128]{1,0:T(8,128)}, f32[128,128]{1,0:T(8,128)S(1)}, u32[]{:S(2)}, u32[]{:S(2)}) collective-permute-start(f32[128,128]{1,0:T(8,128)} %get-tuple-element.34), channel_id=1, source_target_pairs={{0,192},{8,200},{16,208},{24,216},{32,224},{40,232},{48,240},{56,2... | collective-permute-start | bytes 196616 | tf_op jit(solution)/shard_map/ppermute | solution.py:330
  81.3 3.3 %collective-permute-start.18 = (f32[128,128]{1,0:T(8,128)}, f32[128,128]{1,0:T(8,128)S(1)}, u32[]{:S(2)}, u32[]{:S(2)}) collective-permute-start(f32[128,128]{1,0:T(8,128)} %get-tuple-element.35), channel_id=1, source_target_pairs={{0,128},{8,136},{16,144},{24,152},{32,160},{40,168},{48,176},{56,1... | collective-permute-start | bytes 196616 | tf_op jit(solution)/shard_map/ppermute | solution.py:330
  84.6 1.5 %collective-permute-start.19 = (f32[128,128]{1,0:T(8,128)}, f32[128,128]{1,0:T(8,128)S(1)}, u32[]{:S(2)}, u32[]{:S(2)}) collective-permute-start(f32[128,128]{1,0:T(8,128)} %get-tuple-element.36), channel_id=1, source_target_pairs={{0,64},{8,72},{16,80},{24,88},{32,96},{40,104},{48,112},{56,120},{... | collective-permute-start | bytes 196616 | tf_op jit(solution)/shard_map/ppermute | solution.py:330
  86.1 4.9 %shard_map.101 = (f32[128,512]{1,0:T(8,128)}, f32[128,512]{1,0:T(8,128)}) custom-call(s32[32]{0:T(128)} %place_ref.9, s32[32,128]{1,0:T(8,128)} %bitcast.13, f32[32,128]{1,0:T(8,128)} %bitcast.15, f32[1,32]{1,0:T(1,128)} %bitcast.18, f32[128,512]{1,0:T(8,128)} %get-tuple-element.23.g_ref), custom_call_target="tpu_custom_call" | custom-call | tf_op jit(solution)/shard_map/pallas_call | solution.py:349
  91.0 5.0 %shard_map.103.hy_ref = f32[128,512]{1,0:T(8,128)} custom-call(s32[32]{0:T(128)} %place_ref.9, s32[32,128]{1,0:T(8,128)} %bitcast.14, f32[3,7,512]{2,1,0:T(8,128)} %get-tuple-element.22.short_ref, f32[128,512]{1,0:T(8,128)} %get-tuple-element.24.t_ref, f32[128,512]{1,0:T(8,128)} %get-tuple-element.25.f0_ref, f32[128,512]{1,0:T(8,128)} %get-tuple-element.26.own_ref, ...), custom_call_target="tpu_custom_call" | custom-call | tf_op jit(solution)/shard_map/pallas_call | solution.py:390
  96.0 0.0 collective-permute-done.17.a1
  96.0 0.0 collective-permute-done.18.a2
  96.0 1.9 %shard_map.106 = (f32[128,512]{1,0:T(8,128)}, f32[8,128]{1,0:T(8,128)}) custom-call(f32[128,512]{1,0:T(8,128)} %shard_map.103.hy_ref, f32[128,128]{1,0:T(8,128)} %get-tuple-element.33.a0, f32[128,128]{1,0:T(8,128)S(1)} %collective-permute-done.17.a1, f32[128,128]{1,0:T(8,128)S(1)} %collective-permute-done.18.a2, f32[128,128]{1,0:T(8,128)S(1)} %collective-permute-done.19.a3), custom_call_target="tpu_custom_call" | custom-call | tf_op jit(solution)/shard_map/pallas_call | solution.py:393
  98.0 3.0 %collective-permute-start.22 = (f32[8,128]{1,0:T(8,128)}, f32[8,128]{1,0:T(8,128)S(1)}, u32[]{:S(2)}, u32[]{:S(2)}) collective-permute-start(f32[8,128]{1,0:T(8,128)} %get-tuple-element.38), channel_id=1, source_target_pairs={{0,6},{1,7},{2,0},{3,1},{4,2},{5,3},{6,4},{7,5},{8,14},{9,15},{10,... | collective-permute-start | bytes 12296 | tf_op jit(solution)/shard_map/ppermute | solution.py:396
  101.0 2.2 %collective-permute-start.20 = (f32[8,128]{1,0:T(8,128)}, f32[8,128]{1,0:T(8,128)S(1)}, u32[]{:S(2)}, u32[]{:S(2)}) collective-permute-start(f32[8,128]{1,0:T(8,128)} %get-tuple-element.38), channel_id=1, source_target_pairs={{0,4},{1,5},{2,6},{3,7},{4,0},{5,1},{6,2},{7,3},{8,12},{9,13},{10,... | collective-permute-start | bytes 12296 | tf_op jit(solution)/shard_map/ppermute | solution.py:396
  103.2 0.0 collective-permute-done.22
  103.2 2.8 %collective-permute-done.21 = f32[8,128]{1,0:T(8,128)S(1)} collective-permute-done((f32[8,128]{1,0:T(8,128)}, f32[8,128]{1,0:T(8,128)S(1)}, u32[]{:S(2)}, u32[]{:S(2)}) %collective-permute-start.21) | collective-permute-done | bytes 4128 | tf_op jit(solution)/shard_map/ppermute | solution.py:396
  106.0 0.3 collective-permute-done.20
  106.3 0.7 add_add_fusion.sq_ref
  107.0 2.1 %collective-permute-start.23 = (f32[8,128]{1,0:T(8,128)S(1)}, f32[8,128]{1,0:T(8,128)S(1)}, u32[]{:S(2)}, u32[]{:S(2)}) collective-permute-start(f32[8,128]{1,0:T(8,128)S(1)} %add_add_fusion.sq_ref), channel_id=1, source_target_pairs={{0,1},{1,0},{2,3},{3,2},{4,5},{5,4},{6,7},{7,6},{8,9},{9,8},{10,11... | collective-permute-start | bytes 12296 | tf_op jit(solution)/shard_map/ppermute | solution.py:333
  109.1 3.0 %collective-permute-done.23.other_ref = f32[8,128]{1,0:T(8,128)S(1)} collective-permute-done((f32[8,128]{1,0:T(8,128)S(1)}, f32[8,128]{1,0:T(8,128)S(1)}, u32[]{:S(2)}, u32[]{:S(2)}) %collective-permute-start.23) | collective-permute-done | bytes 4128 | tf_op jit(solution)/shard_map/ppermute | solution.py:333
  112.1 1.8 %shard_map.107 = f32[128,512]{1,0:T(8,128)} custom-call(f32[128,512]{1,0:T(8,128)} %get-tuple-element.37.y_ref, f32[8,128]{1,0:T(8,128)} %copy-done.19, f32[8,128]{1,0:T(8,128)S(1)} %collective-permute-done.23.other_ref, f32[1,512]{1,0:T(1,128)} %bitcast.17), custom_call_target="tpu_custom_call" | custom-call | tf_op jit(solution)/shard_map/pallas_call | solution.py:400
  (43 shorter events, 0.2 us)
Async XLA Ops:
  2.1 18.8 %collective-permute-start = (f32[3,128,128]{2,1,0:T(8,128)}, f32[3,128,128]{2,1,0:T(8,128)S(1)}, u32[]{:S(2)}, u32[]{:S(2)}) collective-permute-start(f32[3,128,128]{2,1,0:T(8,128)} %get-tuple-element.30), channel_id=1, source_target_pairs={{0,64},{8,72},{16,80},{24,88},{32,96},{40,104},{48,112},{56,120},{... | collective-permute-start | bytes 589832 | tf_op jit(solution)/shard_map/ppermute | solution.py:330
  5.4 17.3 %collective-permute-start.1 = (f32[3,128,128]{2,1,0:T(8,128)}, f32[3,128,128]{2,1,0:T(8,128)S(1)}, u32[]{:S(2)}, u32[]{:S(2)}) collective-permute-start(f32[3,128,128]{2,1,0:T(8,128)} %get-tuple-element.31), channel_id=1, source_target_pairs={{0,128},{8,136},{16,144},{24,152},{32,160},{40,168},{48,176},{56,1... | collective-permute-start | bytes 589832 | tf_op jit(solution)/shard_map/ppermute | solution.py:330
  10.8 19.9 %collective-permute-start.2 = (f32[3,128,128]{2,1,0:T(8,128)}, f32[3,128,128]{2,1,0:T(8,128)S(1)}, u32[]{:S(2)}, u32[]{:S(2)}) collective-permute-start(f32[3,128,128]{2,1,0:T(8,128)} %get-tuple-element.32), channel_id=1, source_target_pairs={{0,192},{8,200},{16,208},{24,216},{32,224},{40,232},{48,240},{56,2... | collective-permute-start | bytes 589832 | tf_op jit(solution)/shard_map/ppermute | solution.py:330
  16.7 4.2 %copy-start.3 = (f32[3,128,128]{2,1,0:T(8,128)S(1)}, f32[3,128,128]{2,1,0:T(8,128)}, u32[]{:S(2)}) copy-start(f32[3,128,128]{2,1,0:T(8,128)} %get-tuple-element.29.a0) | copy-start | bytes 589828
  16.7 22.0 %all-to-all-start = ((f32[32,24,128]{2,1,0:T(8,128)}), f32[32,24,128]{2,1,0:T(8,128)S(1)}, u32[]{:S(2)}, u32[]{:S(2)}) async-start(f32[32,24,128]{2,1,0:T(8,128)} %bitcast.10), calls=%async_computation | async-start | bytes 786432 | tf_op jit(solution)/shard_map/all_to_all | solution.py:346
  20.9 1.8 %copy-start.4 = (f32[3,128,128]{2,1,0:T(8,128)}, f32[3,128,128]{2,1,0:T(8,128)S(1)}, u32[]{:S(2)}) copy-start(f32[3,128,128]{2,1,0:T(8,128)S(1)} %collective-permute-done.a1) | copy-start | bytes 589828
  22.7 7.9 %copy-start.5 = (f32[3,128,128]{2,1,0:T(8,128)}, f32[3,128,128]{2,1,0:T(8,128)S(1)}, u32[]{:S(2)}) copy-start(f32[3,128,128]{2,1,0:T(8,128)S(1)} %collective-permute-done.1.a2) | copy-start | bytes 589828
  30.6 0.7 copy-start.6
  31.3 0.7 copy-start.1
  31.3 19.0 %collective-permute-start.9 = (f32[4,128,128]{2,1,0:T(8,128)S(1)}, f32[4,128,128]{2,1,0:T(8,128)S(1)}, u32[]{:S(2)}, u32[]{:S(2)}) collective-permute-start(f32[4,128,128]{2,1,0:T(8,128)S(1)} %pad_maximum_fusion.rest_0_), channel_id=1, source_target_pairs={{0,32},{8,40},{16,48},{24,56},{32,0},{40,8},{48,16},{56,24},{64,96... | collective-permute-start | bytes 786440 | tf_op jit(solution)/shard_map/ppermute | solution.py:333
  31.3 19.1 %collective-permute-start.5 = (f32[4,128,128]{2,1,0:T(8,128)S(1)}, f32[4,128,128]{2,1,0:T(8,128)S(1)}, u32[]{:S(2)}, u32[]{:S(2)}) collective-permute-start(f32[4,128,128]{2,1,0:T(8,128)S(1)} %pad_maximum_fusion.rest_0_), channel_id=1, source_target_pairs={{0,16},{8,24},{16,0},{24,8},{32,48},{40,56},{48,32},{56,40},{64,80... | collective-permute-start | bytes 786440 | tf_op jit(solution)/shard_map/ppermute | solution.py:333
  31.7 19.4 %collective-permute-start.3 = (f32[4,128,128]{2,1,0:T(8,128)S(1)}, f32[4,128,128]{2,1,0:T(8,128)S(1)}, u32[]{:S(2)}, u32[]{:S(2)}) collective-permute-start(f32[4,128,128]{2,1,0:T(8,128)S(1)} %pad_maximum_fusion.rest_0_), channel_id=1, source_target_pairs={{0,8},{8,0},{16,24},{24,16},{32,40},{40,32},{48,56},{56,48},{64,72... | collective-permute-start | bytes 786440 | tf_op jit(solution)/shard_map/ppermute | solution.py:333
  32.0 18.3 %copy-start.2 = (f32[4,128,128]{2,1,0:T(8,128)}, f32[4,128,128]{2,1,0:T(8,128)S(1)}, u32[]{:S(2)}) copy-start(f32[4,128,128]{2,1,0:T(8,128)S(1)} %pad_maximum_fusion.1.rest_1_) | copy-start | bytes 786436
  32.0 19.2 %collective-permute-start.6 = (f32[4,128,128]{2,1,0:T(8,128)S(1)}, f32[4,128,128]{2,1,0:T(8,128)S(1)}, u32[]{:S(2)}, u32[]{:S(2)}) collective-permute-start(f32[4,128,128]{2,1,0:T(8,128)S(1)} %pad_maximum_fusion.1.rest_1_), channel_id=1, source_target_pairs={{0,16},{8,24},{16,0},{24,8},{32,48},{40,56},{48,32},{56,40},{64,80... | collective-permute-start | bytes 786440 | tf_op jit(solution)/shard_map/ppermute | solution.py:333
  38.7 0.8 copy-start
  41.3 49.6 %all-to-all-start.1 = ((f32[32,24,128]{2,1,0:T(8,128)}), f32[32,24,128]{2,1,0:T(8,128)S(1)}, u32[]{:S(2)}, u32[]{:S(2)}) async-start(f32[32,24,128]{2,1,0:T(8,128)} %shard_map.102), calls=%async_computation.1 | async-start | bytes 786432 | tf_op jit(solution)/shard_map/all_to_all | solution.py:366
  48.8 17.1 %collective-permute-start.10 = (f32[4,128,128]{2,1,0:T(8,128)S(1)}, f32[4,128,128]{2,1,0:T(8,128)S(1)}, u32[]{:S(2)}, u32[]{:S(2)}) collective-permute-start(f32[4,128,128]{2,1,0:T(8,128)S(1)} %pad_maximum_fusion.1.rest_1_), channel_id=1, source_target_pairs={{0,32},{8,40},{16,48},{24,56},{32,0},{40,8},{48,16},{56,24},{64,96... | collective-permute-start | bytes 786440 | tf_op jit(solution)/shard_map/ppermute | solution.py:333
  50.4 22.2 %copy-start.7 = (f32[4,128,128]{2,1,0:T(8,128)}, f32[4,128,128]{2,1,0:T(8,128)S(1)}, u32[]{:S(2)}) copy-start(f32[4,128,128]{2,1,0:T(8,128)S(1)} %collective-permute-done.9.rest_8_) | copy-start | bytes 786436
  50.4 15.6 %collective-permute-start.4 = (f32[4,128,128]{2,1,0:T(8,128)S(1)}, f32[4,128,128]{2,1,0:T(8,128)S(1)}, u32[]{:S(2)}, u32[]{:S(2)}) collective-permute-start(f32[4,128,128]{2,1,0:T(8,128)S(1)} %pad_maximum_fusion.1.rest_1_), channel_id=1, source_target_pairs={{0,8},{8,0},{16,24},{24,16},{32,40},{40,32},{48,56},{56,48},{64,72... | collective-permute-start | bytes 786440 | tf_op jit(solution)/shard_map/ppermute | solution.py:333
  50.5 22.1 %copy-start.8 = (f32[4,128,128]{2,1,0:T(8,128)}, f32[4,128,128]{2,1,0:T(8,128)S(1)}, u32[]{:S(2)}) copy-start(f32[4,128,128]{2,1,0:T(8,128)S(1)} %collective-permute-done.5.rest_4_) | copy-start | bytes 786436
  50.5 16.0 %collective-permute-start.13 = (f32[4,128,128]{2,1,0:T(8,128)S(1)}, f32[4,128,128]{2,1,0:T(8,128)S(1)}, u32[]{:S(2)}, u32[]{:S(2)}) collective-permute-start(f32[4,128,128]{2,1,0:T(8,128)S(1)} %collective-permute-done.9.rest_8_), channel_id=1, source_target_pairs={{0,16},{8,24},{16,0},{24,8},{32,48},{40,56},{48,32},{56,40},{64,80... | collective-permute-start | bytes 786440 | tf_op jit(solution)/shard_map/ppermute | solution.py:333
  51.1 21.4 %copy-start.9 = (f32[4,128,128]{2,1,0:T(8,128)}, f32[4,128,128]{2,1,0:T(8,128)S(1)}, u32[]{:S(2)}) copy-start(f32[4,128,128]{2,1,0:T(8,128)S(1)} %collective-permute-done.3.rest_2_) | copy-start | bytes 786436
  51.1 15.4 %collective-permute-start.11 = (f32[4,128,128]{2,1,0:T(8,128)S(1)}, f32[4,128,128]{2,1,0:T(8,128)S(1)}, u32[]{:S(2)}, u32[]{:S(2)}) collective-permute-start(f32[4,128,128]{2,1,0:T(8,128)S(1)} %collective-permute-done.9.rest_8_), channel_id=1, source_target_pairs={{0,8},{8,0},{16,24},{24,16},{32,40},{40,32},{48,56},{56,48},{64,72... | collective-permute-start | bytes 786440 | tf_op jit(solution)/shard_map/ppermute | solution.py:333
  51.2 21.3 %copy-start.10 = (f32[4,128,128]{2,1,0:T(8,128)}, f32[4,128,128]{2,1,0:T(8,128)S(1)}, u32[]{:S(2)}) copy-start(f32[4,128,128]{2,1,0:T(8,128)S(1)} %collective-permute-done.6.rest_5_) | copy-start | bytes 786436
  51.2 19.7 %collective-permute-start.14 = (f32[4,128,128]{2,1,0:T(8,128)S(1)}, f32[4,128,128]{2,1,0:T(8,128)S(1)}, u32[]{:S(2)}, u32[]{:S(2)}) collective-permute-start(f32[4,128,128]{2,1,0:T(8,128)S(1)} %collective-permute-done.6.rest_5_), channel_id=1, source_target_pairs={{0,32},{8,40},{16,48},{24,56},{32,0},{40,8},{48,16},{56,24},{64,96... | collective-permute-start | bytes 786440 | tf_op jit(solution)/shard_map/ppermute | solution.py:333
  65.9 6.6 %copy-start.11 = (f32[4,128,128]{2,1,0:T(8,128)}, f32[4,128,128]{2,1,0:T(8,128)S(1)}, u32[]{:S(2)}) copy-start(f32[4,128,128]{2,1,0:T(8,128)S(1)} %collective-permute-done.10.rest_9_) | copy-start | bytes 786436
  65.9 5.1 %collective-permute-start.8 = (f32[4,128,128]{2,1,0:T(8,128)S(1)}, f32[4,128,128]{2,1,0:T(8,128)S(1)}, u32[]{:S(2)}, u32[]{:S(2)}) collective-permute-start(f32[4,128,128]{2,1,0:T(8,128)S(1)} %collective-permute-done.6.rest_5_), channel_id=1, source_target_pairs={{0,8},{8,0},{16,24},{24,16},{32,40},{40,32},{48,56},{56,48},{64,72... | collective-permute-start | bytes 786440 | tf_op jit(solution)/shard_map/ppermute | solution.py:333
  65.9 6.6 %copy-start.12 = (f32[4,128,128]{2,1,0:T(8,128)}, f32[4,128,128]{2,1,0:T(8,128)S(1)}, u32[]{:S(2)}) copy-start(f32[4,128,128]{2,1,0:T(8,128)S(1)} %collective-permute-done.4.rest_3_) | copy-start | bytes 786436
  66.0 5.0 %collective-permute-start.7 = (f32[4,128,128]{2,1,0:T(8,128)S(1)}, f32[4,128,128]{2,1,0:T(8,128)S(1)}, u32[]{:S(2)}, u32[]{:S(2)}) collective-permute-start(f32[4,128,128]{2,1,0:T(8,128)S(1)} %collective-permute-done.5.rest_4_), channel_id=1, source_target_pairs={{0,8},{8,0},{16,24},{24,16},{32,40},{40,32},{48,56},{56,48},{64,72... | collective-permute-start | bytes 786440 | tf_op jit(solution)/shard_map/ppermute | solution.py:333
  66.5 6.1 %copy-start.13 = (f32[4,128,128]{2,1,0:T(8,128)}, f32[4,128,128]{2,1,0:T(8,128)S(1)}, u32[]{:S(2)}) copy-start(f32[4,128,128]{2,1,0:T(8,128)S(1)} %collective-permute-done.13.rest_12_) | copy-start | bytes 786436
  66.5 4.5 %collective-permute-start.12 = (f32[4,128,128]{2,1,0:T(8,128)S(1)}, f32[4,128,128]{2,1,0:T(8,128)S(1)}, u32[]{:S(2)}, u32[]{:S(2)}) collective-permute-start(f32[4,128,128]{2,1,0:T(8,128)S(1)} %collective-permute-done.10.rest_9_), channel_id=1, source_target_pairs={{0,8},{8,0},{16,24},{24,16},{32,40},{40,32},{48,56},{56,48},{64,72... | collective-permute-start | bytes 786440 | tf_op jit(solution)/shard_map/ppermute | solution.py:333
  66.6 6.0 %copy-start.14 = (f32[4,128,128]{2,1,0:T(8,128)}, f32[4,128,128]{2,1,0:T(8,128)S(1)}, u32[]{:S(2)}) copy-start(f32[4,128,128]{2,1,0:T(8,128)S(1)} %collective-permute-done.11.rest_10_) | copy-start | bytes 786436
  66.6 4.5 %collective-permute-start.15 = (f32[4,128,128]{2,1,0:T(8,128)S(1)}, f32[4,128,128]{2,1,0:T(8,128)S(1)}, u32[]{:S(2)}, u32[]{:S(2)}) collective-permute-start(f32[4,128,128]{2,1,0:T(8,128)S(1)} %collective-permute-done.13.rest_12_), channel_id=1, source_target_pairs={{0,8},{8,0},{16,24},{24,16},{32,40},{40,32},{48,56},{56,48},{64,72... | collective-permute-start | bytes 786440 | tf_op jit(solution)/shard_map/ppermute | solution.py:333
  71.0 1.6 %copy-start.15 = (f32[4,128,128]{2,1,0:T(8,128)}, f32[4,128,128]{2,1,0:T(8,128)S(1)}, u32[]{:S(2)}) copy-start(f32[4,128,128]{2,1,0:T(8,128)S(1)} %collective-permute-done.14.rest_13_) | copy-start | bytes 786436
  71.0 1.5 %collective-permute-start.16 = (f32[4,128,128]{2,1,0:T(8,128)S(1)}, f32[4,128,128]{2,1,0:T(8,128)S(1)}, u32[]{:S(2)}, u32[]{:S(2)}) collective-permute-start(f32[4,128,128]{2,1,0:T(8,128)S(1)} %collective-permute-done.14.rest_13_), channel_id=1, source_target_pairs={{0,8},{8,0},{16,24},{24,16},{32,40},{40,32},{48,56},{56,48},{64,72... | collective-permute-start | bytes 786440 | tf_op jit(solution)/shard_map/ppermute | solution.py:333
  71.0 0.7 copy-start.17
  71.0 0.8 copy-start.18
  71.0 0.9 copy-start.16
  78.6 17.4 %collective-permute-start.17 = (f32[128,128]{1,0:T(8,128)}, f32[128,128]{1,0:T(8,128)S(1)}, u32[]{:S(2)}, u32[]{:S(2)}) collective-permute-start(f32[128,128]{1,0:T(8,128)} %get-tuple-element.34), channel_id=1, source_target_pairs={{0,192},{8,200},{16,208},{24,216},{32,224},{40,232},{48,240},{56,2... | collective-permute-start | bytes 196616 | tf_op jit(solution)/shard_map/ppermute | solution.py:330
  81.3 14.7 %collective-permute-start.18 = (f32[128,128]{1,0:T(8,128)}, f32[128,128]{1,0:T(8,128)S(1)}, u32[]{:S(2)}, u32[]{:S(2)}) collective-permute-start(f32[128,128]{1,0:T(8,128)} %get-tuple-element.35), channel_id=1, source_target_pairs={{0,128},{8,136},{16,144},{24,152},{32,160},{40,168},{48,176},{56,1... | collective-permute-start | bytes 196616 | tf_op jit(solution)/shard_map/ppermute | solution.py:330
  84.6 11.4 %collective-permute-start.19 = (f32[128,128]{1,0:T(8,128)}, f32[128,128]{1,0:T(8,128)S(1)}, u32[]{:S(2)}, u32[]{:S(2)}) collective-permute-start(f32[128,128]{1,0:T(8,128)} %get-tuple-element.36), channel_id=1, source_target_pairs={{0,64},{8,72},{16,80},{24,88},{32,96},{40,104},{48,112},{56,120},{... | collective-permute-start | bytes 196616 | tf_op jit(solution)/shard_map/ppermute | solution.py:330
  98.0 5.2 %collective-permute-start.22 = (f32[8,128]{1,0:T(8,128)}, f32[8,128]{1,0:T(8,128)S(1)}, u32[]{:S(2)}, u32[]{:S(2)}) collective-permute-start(f32[8,128]{1,0:T(8,128)} %get-tuple-element.38), channel_id=1, source_target_pairs={{0,6},{1,7},{2,0},{3,1},{4,2},{5,3},{6,4},{7,5},{8,14},{9,15},{10,... | collective-permute-start | bytes 12296 | tf_op jit(solution)/shard_map/ppermute | solution.py:396
  101.0 5.0 %collective-permute-start.21 = (f32[8,128]{1,0:T(8,128)}, f32[8,128]{1,0:T(8,128)S(1)}, u32[]{:S(2)}, u32[]{:S(2)}) collective-permute-start(f32[8,128]{1,0:T(8,128)} %get-tuple-element.38), channel_id=1, source_target_pairs={{0,2},{1,3},{2,4},{3,5},{4,6},{5,7},{6,0},{7,1},{8,10},{9,11},{10,... | collective-permute-start | bytes 12296 | tf_op jit(solution)/shard_map/ppermute | solution.py:396
  101.0 5.3 %collective-permute-start.20 = (f32[8,128]{1,0:T(8,128)}, f32[8,128]{1,0:T(8,128)S(1)}, u32[]{:S(2)}, u32[]{:S(2)}) collective-permute-start(f32[8,128]{1,0:T(8,128)} %get-tuple-element.38), channel_id=1, source_target_pairs={{0,4},{1,5},{2,6},{3,7},{4,0},{5,1},{6,2},{7,3},{8,12},{9,13},{10,... | collective-permute-start | bytes 12296 | tf_op jit(solution)/shard_map/ppermute | solution.py:396
  107.0 5.1 %copy-start.19 = (f32[8,128]{1,0:T(8,128)}, f32[8,128]{1,0:T(8,128)S(1)}, u32[]{:S(2)}) copy-start(f32[8,128]{1,0:T(8,128)S(1)} %add_add_fusion.sq_ref) | copy-start | bytes 12292
  107.0 5.1 %collective-permute-start.23 = (f32[8,128]{1,0:T(8,128)S(1)}, f32[8,128]{1,0:T(8,128)S(1)}, u32[]{:S(2)}, u32[]{:S(2)}) collective-permute-start(f32[8,128]{1,0:T(8,128)S(1)} %add_add_fusion.sq_ref), channel_id=1, source_target_pairs={{0,1},{1,0},{2,3},{3,2},{4,5},{5,4},{6,7},{7,6},{8,9},{9,8},{10,11... | collective-permute-start | bytes 12296 | tf_op jit(solution)/shard_map/ppermute | solution.py:333

commit v2 on v1

--- a/solution.py
+++ b/solution.py
@@ -228,7 +228,8 @@
 def attend_kernel(
     place_ref, doc_ref, a0, a1, a2, a3, *rest
 ):
-    kv, late, rest = rest[:14], rest[14:16], rest[16:]
+    kv, late, rest = rest[:12], rest[12:16], rest[16:]
+    late = {(3, 0): late[0], (5, 1): late[1], (7, 0): late[2], (7, 1): late[3]}
     outs, (q_ref, kv_ref, sem, k_ref, v_ref, s_ref, qs_ref, p_ref) = rest[:4], rest[4:]
     copies = []
 
@@ -236,8 +237,9 @@
         copies.append(pltpu.make_async_copy(src, dst, sem.at[len(copies)]))
         copies[-1].start()
 
-    for n, ref in enumerate(kv):
-        fetch(ref, kv_ref.at[n // 2, n % 2])
+    early = [(x, t) for x in range(8) for t in range(2) if (x, t) not in late]
+    for (x, t), ref in zip(early, kv):
+        fetch(ref, kv_ref.at[x, t])
     for i, ref in enumerate((a0, a1, a2, a3)):
         fetch(ref.at[0], q_ref.at[i])
     me = lax.axis_index("seq")
@@ -245,39 +247,41 @@
     g = lax.rem(me, 8)
 
     for x in range(8):
-        if x < 7:
-            copies[2 * x].wait()
-            copies[2 * x + 1].wait()
+        for t in range(2):
+            if (x, t) in early:
+                copies[early.index((x, t))].wait()
         for k in range(4):
             at = place_ref[lax.rem(zq + 4 - k, 4) * 8 + lax.bitwise_xor(g, x)]
             rows = pl.ds(pl.multiple_of(at * T, T), T)
-            k_ref[rows, :HD], k_ref[rows, HD:] = split(kv_ref[x, 0, k] if x < 7 else late[0][k])
-            v_ref[rows, :HD], v_ref[rows, HD:] = split(kv_ref[x, 1, k] if x < 7 else late[1][k])
-    for copy in copies[14:]:
+            k_ref[rows, :HD], k_ref[rows, HD:] = split(late[x, 0][k] if (x, 0) in late else kv_ref[x, 0, k])
+            v_ref[rows, :HD], v_ref[rows, HD:] = split(late[x, 1][k] if (x, 1) in late else kv_ref[x, 1, k])
+    for copy in copies[12:]:
         copy.wait()
     scale = 1.0 / jnp.sqrt(jnp.float32(HD))
-    ahead = iota((T, T), 1) - iota((T, T), 0)
+    causal = iota((T, T), 1) <= iota((T, T), 0)
     home = [place_ref[lax.rem(zq + 4 - i, 4) * 8 + g] for i in range(4)]
     first = [jnp.maximum(c - (NB - 1), 0) for c in home]
     window = [pl.ds(pl.multiple_of(f * T, T), NB * T) for f in first]
 
     def score(i):
-        high, low = split(q_ref[i])
+        high, low = split(q_ref[i] * scale)
         qs_ref[i, :T, :HD], qs_ref[i, :T, HD:] = high, high
         qs_ref[i, T:, :HD], qs_ref[i, T:, HD:] = low, jnp.zeros_like(low)
         both = dot(qs_ref[i], k_ref[window[i], :], ((1,), (1,)))
-        s_ref[i % 2] = (both[:T] + both[T:]) * scale
+        s_ref[i % 2] = both[:T] + both[T:]
 
     score(0)
     for i in range(4):
         if i < 3:
             score(i + 1)
         col = column(doc_row(doc_ref, home[i]))
+        own = pl.ds(pl.multiple_of((home[i] - first[i]) * T, T), T)
+        s_ref[i % 2, :, own] = jnp.where(causal, s_ref[i % 2, :, own], -1e30)
         top = None
         for n in range(NB):
             cols = slice(n * T, n * T + T)
-            allowed = (doc_row(doc_ref, first[i] + n) == col) & (ahead <= (home[i] - first[i] - n) * T)
-            s = jnp.where(allowed, s_ref[i % 2, :, cols], -1e30)
+            docs = jnp.where(first[i] + n <= home[i], doc_row(doc_ref, first[i] + n), -1.0)
+            s = jnp.where(docs == col, s_ref[i % 2, :, cols], -1e30)
             s_ref[i % 2, :, cols] = s
             top = s if top is None else jnp.maximum(top, s)
         top = jnp.max(top, axis=1, keepdims=True)
@@ -361,22 +365,22 @@
     cdk, cdv = swap(dk, "seq", 1), swap(dv, "seq", 1)
 
     chosen = call(select_kernel, [(N, 24, 128)], [SMEM, VMEM], [pltpu.SMEM((N,), jnp.int32)])(
-        placement_list, hbm(pieces)
+        placement_list, vmem(pieces)
     )
     back = lax.all_to_all(chosen, "seq", 0, 0, tiled=True).reshape(96, 8, 128)
 
     bf = jnp.bfloat16
-    pieces_kv = (k0, v0, ck, cv, xk, xv, cxk, cxv, zk, zv, czk, czv, dk, dv, cdk, cdv)
-    near = [hbm(a) for a in (*held[1:], *pieces_kv[:14])]
-    near += [vmem(cdk), vmem(cdv)]
+    pieces_kv = (k0, v0, ck, cv, xk, xv, cxv, zk, zv, czk, dk, dv)
+    near = [hbm(a) for a in (*held[1:], *pieces_kv)]
+    near += [vmem(a) for a in (cxk, czv, cdk, cdv)]
     attended = call(
         attend_kernel,
         [(T, HD)] * 4,
-        [SMEM, VMEM] + [ANY] * 18 + [VMEM] * 2,
+        [SMEM, VMEM] + [ANY] * 16 + [VMEM] * 4,
         [
             pltpu.VMEM((4, T, HD), F32),
             pltpu.VMEM((7, 2, 4, T, HD), F32),
-            pltpu.SemaphoreType.DMA((18,)),
+            pltpu.SemaphoreType.DMA((16,)),
             *[pltpu.VMEM((N * T, 2 * HD), bf)] * 2,
             pltpu.VMEM((2, T, NB * T), F32),
             pltpu.VMEM((4, 2 * T, 2 * HD), bf),

time: 115 us -> 113 us (0.983)
    unnamed x40 -> x34, local copies, waits for them, and re-layouts: 2.56 us -> 1.67 us
where the time goes in v2:
time: 113 us
  starting transfers between devices  43.5 us (38%)
  waiting for transfers between devices  40.1 us (35%)
  Pallas kernels  26.3 us (23%)
  local copies, waits for them, and re-layouts  1.71 us (2%)
    ppermute x15, waiting for transfers between devices, swap(): lax.ppermute(x, axis, [(b, b ^ bit) for b in range(N if axis == 'seq' els...  22.1 us
    ppermute x6, starting transfers between devices, ring(): return lax.ppermute(x, 'seq', [(b, (b + 8 * k) % N) for b in range(N)])  18.8 us
    ppermute x6, waiting for transfers between devices, ring(): return lax.ppermute(x, 'seq', [(b, (b + 8 * k) % N) for b in range(N)])  9.71 us
    ppermute x15, starting transfers between devices, swap(): lax.ppermute(x, axis, [(b, b ^ bit) for b in range(N if axis == 'seq' els...  7.82 us
    all_to_all x1, starting transfers between devices, per_device(): back = lax.all_to_all(chosen, 'seq', 0, 0, tiled=True).reshape(96, 8, 128)  7.44 us
    pallas_call x1, Pallas kernels, per_device(): call(attend_kernel, [(T, HD)] * 4, [SMEM, VMEM] + [ANY] * 16 + [VMEM] * 4...  5.81 us
    ppermute x3, starting transfers between devices, along_y(): return lax.ppermute(squares, 'mp', [(m, (m + 2 * k) % 8) for m in range(8)])  5.22 us
    all_to_all x1, waiting for transfers between devices, per_device(): pieces = lax.all_to_all(tiles.reshape(N, 24, 128), 'seq', 0, 0, tiled=True)  5.21 us
  transfers between devices with their start and end apart: 26, of which 9 were waited for; matrix products, arithmetic and copies ran while one was open for 0% of the time, Pallas kernels for 18%

profile of v2, /device:TPU:2, one launch (start us, length us, event | category | flops | bytes accessed | tf_op | source)
XLA Modules:
  0.0 112.6 jit_solution(450871008989476855)
XLA Ops:
  0.0 2.1 %shard_map.104 = (f32[3,128,128]{2,1,0:T(8,128)}, f32[3,128,128]{2,1,0:T(8,128)}, f32[3,128,128]{2,1,0:T(8,128)}, f32[3,128,128]{2,1,0:T(8,128)}) custom-call(f32[128,512]{1,0:T(8,128)} %q_ref.1, f32[128,512]{1,0:T(8,128)} %k_ref.1, f32[128,512]{1,0:T(8,128)} %v_ref.1), custom_call_target="tpu_custom_call" | custom-call | tf_op jit(solution)/shard_map/pallas_call | solution.py:339
  2.1 3.3 %collective-permute-start = (f32[3,128,128]{2,1,0:T(8,128)}, f32[3,128,128]{2,1,0:T(8,128)S(1)}, u32[]{:S(2)}, u32[]{:S(2)}) collective-permute-start(f32[3,128,128]{2,1,0:T(8,128)} %get-tuple-element.30), channel_id=1, source_target_pairs={{0,64},{8,72},{16,80},{24,88},{32,96},{40,104},{48,112},{56,120},{... | collective-permute-start | bytes 589832 | tf_op jit(solution)/shard_map/ppermute | solution.py:334
  5.4 5.4 %collective-permute-start.1 = (f32[3,128,128]{2,1,0:T(8,128)}, f32[3,128,128]{2,1,0:T(8,128)S(1)}, u32[]{:S(2)}, u32[]{:S(2)}) collective-permute-start(f32[3,128,128]{2,1,0:T(8,128)} %get-tuple-element.31), channel_id=1, source_target_pairs={{0,128},{8,136},{16,144},{24,152},{32,160},{40,168},{48,176},{56,1... | collective-permute-start | bytes 589832 | tf_op jit(solution)/shard_map/ppermute | solution.py:334
  10.8 2.7 %collective-permute-start.2 = (f32[3,128,128]{2,1,0:T(8,128)}, f32[3,128,128]{2,1,0:T(8,128)S(1)}, u32[]{:S(2)}, u32[]{:S(2)}) collective-permute-start(f32[3,128,128]{2,1,0:T(8,128)} %get-tuple-element.32), channel_id=1, source_target_pairs={{0,192},{8,200},{16,208},{24,216},{32,224},{40,232},{48,240},{56,2... | collective-permute-start | bytes 589832 | tf_op jit(solution)/shard_map/ppermute | solution.py:334
  13.4 3.2 %shard_map.100 = (f32[96,8,128]{2,1,0:T(8,128)}, f32[128,512]{1,0:T(8,128)}, f32[128,512]{1,0:T(8,128)}, f32[2,8,512]{2,1,0:T(8,128)}, f32[3,7,512]{2,1,0:T(8,128)}) custom-call(s32[32]{0:T(128)} %place_ref.9, s32[32,128]{1,0:T(8,128)} %bitcast.11, f32[3,128,512]{2,1,0:T(8,128)} %bitcast.9, f32[3,7,32]{2,1,0:T(8,128)} %bitcast.16), custom_call_target="tpu_custom_call" | custom-call | tf_op jit(solution)/shard_map/pallas_call | solution.py:344
  16.7 4.2 %all-to-all-start = ((f32[32,24,128]{2,1,0:T(8,128)}), f32[32,24,128]{2,1,0:T(8,128)S(1)}, u32[]{:S(2)}, u32[]{:S(2)}) async-start(f32[32,24,128]{2,1,0:T(8,128)} %bitcast.10), calls=%async_computation | async-start | bytes 786432 | tf_op jit(solution)/shard_map/all_to_all | solution.py:350
  20.9 0.0 collective-permute-done.a1
  21.0 1.8 %collective-permute-done.1.a2 = f32[3,128,128]{2,1,0:T(8,128)S(1)} collective-permute-done((f32[3,128,128]{2,1,0:T(8,128)}, f32[3,128,128]{2,1,0:T(8,128)S(1)}, u32[]{:S(2)}, u32[]{:S(2)}) %collective-permute-start.1) | collective-permute-done | bytes 196640 | tf_op jit(solution)/shard_map/ppermute | solution.py:334
  22.8 7.9 %collective-permute-done.2.a3 = f32[3,128,128]{2,1,0:T(8,128)S(1)} collective-permute-done((f32[3,128,128]{2,1,0:T(8,128)}, f32[3,128,128]{2,1,0:T(8,128)S(1)}, u32[]{:S(2)}, u32[]{:S(2)}) %collective-permute-start.2) | collective-permute-done | bytes 196640 | tf_op jit(solution)/shard_map/ppermute | solution.py:334
  30.7 0.6 copy-done.5
  31.4 0.0 collective-permute-start.8
  31.4 0.4 collective-permute-start.5
  31.8 0.0 collective-permute-start.3
  31.8 0.2 copy-done
  32.1 1.5 %collective-permute-start.6 = (f32[4,128,128]{2,1,0:T(8,128)S(1)}, f32[4,128,128]{2,1,0:T(8,128)S(1)}, u32[]{:S(2)}, u32[]{:S(2)}) collective-permute-start(f32[4,128,128]{2,1,0:T(8,128)S(1)} %pad_maximum_fusion.1.rest_1_), channel_id=1, source_target_pairs={{0,16},{8,24},{16,0},{24,8},{32,48},{40,56},{48,32},{56,40},{64,80... | collective-permute-start | bytes 786440 | tf_op jit(solution)/shard_map/ppermute | solution.py:337
  33.5 5.2 %all-to-all-done.r_ref = f32[32,24,128]{2,1,0:T(8,128)S(1)} async-done(((f32[32,24,128]{2,1,0:T(8,128)}), f32[32,24,128]{2,1,0:T(8,128)S(1)}, u32[]{:S(2)}, u32[]{:S(2)}) %all-to-all-start) | async-done | bytes 393248 | tf_op jit(solution)/shard_map/all_to_all | solution.py:350
  38.7 1.5 %shard_map.102 = f32[32,24,128]{2,1,0:T(8,128)} custom-call(s32[32]{0:T(128)} %place_ref.9, f32[32,24,128]{2,1,0:T(8,128)S(1)} %all-to-all-done.r_ref), custom_call_target="tpu_custom_call" | custom-call | tf_op jit(solution)/shard_map/pallas_call | solution.py:367
  40.3 7.4 %all-to-all-start.1 = ((f32[32,24,128]{2,1,0:T(8,128)}), f32[32,24,128]{2,1,0:T(8,128)S(1)}, u32[]{:S(2)}, u32[]{:S(2)}) async-start(f32[32,24,128]{2,1,0:T(8,128)} %shard_map.102), calls=%async_computation.1 | async-start | bytes 786432 | tf_op jit(solution)/shard_map/all_to_all | solution.py:370
  47.7 1.6 %collective-permute-start.9 = (f32[4,128,128]{2,1,0:T(8,128)S(1)}, f32[4,128,128]{2,1,0:T(8,128)S(1)}, u32[]{:S(2)}, u32[]{:S(2)}) collective-permute-start(f32[4,128,128]{2,1,0:T(8,128)S(1)} %pad_maximum_fusion.1.rest_1_), channel_id=1, source_target_pairs={{0,32},{8,40},{16,48},{24,56},{32,0},{40,8},{48,16},{56,24},{64,96... | collective-permute-start | bytes 786440 | tf_op jit(solution)/shard_map/ppermute | solution.py:337
  49.3 0.0 collective-permute-done.8.rest_7_
  49.3 0.1 collective-permute-start.4
  49.4 0.0 collective-permute-done.5.rest_4_
  49.4 0.6 collective-permute-start.11
  50.0 0.0 collective-permute-done.3.rest_2_
  50.0 0.1 collective-permute-start.10
  50.1 0.0 collective-permute-done.6.rest_5_
  50.2 0.4 collective-permute-start.12
  50.5 14.3 %collective-permute-done.9.rest_8_ = f32[4,128,128]{2,1,0:T(8,128)S(1)} collective-permute-done((f32[4,128,128]{2,1,0:T(8,128)S(1)}, f32[4,128,128]{2,1,0:T(8,128)S(1)}, u32[]{:S(2)}, u32[]{:S(2)}) %collective-permute-start.9) | collective-permute-done | bytes 262176 | tf_op jit(solution)/shard_map/ppermute | solution.py:337
  64.8 0.0 collective-permute-start.7
  64.8 0.0 collective-permute-done.4.rest_3_
  64.9 0.5 collective-permute-start.13
  65.4 0.0 collective-permute-done.11.rest_10_
  65.4 0.1 collective-permute-start.14
  65.5 0.0 collective-permute-done.10.rest_9_
  65.5 0.4 collective-permute-start.15
  65.9 4.0 %collective-permute-done.12.rest_11_ = f32[4,128,128]{2,1,0:T(8,128)S(1)} collective-permute-done((f32[4,128,128]{2,1,0:T(8,128)S(1)}, f32[4,128,128]{2,1,0:T(8,128)S(1)}, u32[]{:S(2)}, u32[]{:S(2)}) %collective-permute-start.12) | collective-permute-done | bytes 262176 | tf_op jit(solution)/shard_map/ppermute | solution.py:337
  69.9 0.0 collective-permute-start.16
  69.9 0.0 collective-permute-done.13.rest_12_
  69.9 0.0 collective-permute-done.14.rest_13_
  69.9 0.0 collective-permute-done.7.rest_6_
  69.9 0.0 collective-permute-done.15.rest_14_
  69.9 0.6 copy-done.14
  70.6 0.1 copy-done.15
  70.7 0.7 collective-permute-done.16.rest_15_
  71.5 5.8 %shard_map.105 = (f32[128,128]{1,0:T(8,128)}, f32[128,128]{1,0:T(8,128)}, f32[128,128]{1,0:T(8,128)}, f32[128,128]{1,0:T(8,128)}) custom-call(s32[32]{0:T(128)} %place_ref.9, s32[32,128]{1,0:T(8,128)} %bitcast.12, f32[3,128,128]{2,1,0:T(8,128)} %get-tuple-element.29.a0, f32[3,128,128]{2,1,0:T(8,128)} %copy-done.3, f32[3,128,128]{2,1,0:T(8,128)} %copy-done.4, ...), custom_call_target="tpu_custom_call" | custom-call | tf_op jit(solution)/shard_map/pallas_call | solution.py:376
  77.3 2.7 %collective-permute-start.17 = (f32[128,128]{1,0:T(8,128)}, f32[128,128]{1,0:T(8,128)S(1)}, u32[]{:S(2)}, u32[]{:S(2)}) collective-permute-start(f32[128,128]{1,0:T(8,128)} %get-tuple-element.34), channel_id=1, source_target_pairs={{0,192},{8,200},{16,208},{24,216},{32,224},{40,232},{48,240},{56,2... | collective-permute-start | bytes 196616 | tf_op jit(solution)/shard_map/ppermute | solution.py:334
  80.1 3.3 %collective-permute-start.18 = (f32[128,128]{1,0:T(8,128)}, f32[128,128]{1,0:T(8,128)S(1)}, u32[]{:S(2)}, u32[]{:S(2)}) collective-permute-start(f32[128,128]{1,0:T(8,128)} %get-tuple-element.35), channel_id=1, source_target_pairs={{0,128},{8,136},{16,144},{24,152},{32,160},{40,168},{48,176},{56,1... | collective-permute-start | bytes 196616 | tf_op jit(solution)/shard_map/ppermute | solution.py:334
  83.3 1.5 %collective-permute-start.19 = (f32[128,128]{1,0:T(8,128)}, f32[128,128]{1,0:T(8,128)S(1)}, u32[]{:S(2)}, u32[]{:S(2)}) collective-permute-start(f32[128,128]{1,0:T(8,128)} %get-tuple-element.36), channel_id=1, source_target_pairs={{0,64},{8,72},{16,80},{24,88},{32,96},{40,104},{48,112},{56,120},{... | collective-permute-start | bytes 196616 | tf_op jit(solution)/shard_map/ppermute | solution.py:334
  84.8 4.9 %shard_map.101 = (f32[128,512]{1,0:T(8,128)}, f32[128,512]{1,0:T(8,128)}) custom-call(s32[32]{0:T(128)} %place_ref.9, s32[32,128]{1,0:T(8,128)} %bitcast.13, f32[32,128]{1,0:T(8,128)} %bitcast.15, f32[1,32]{1,0:T(1,128)} %bitcast.18, f32[128,512]{1,0:T(8,128)} %get-tuple-element.23.g_ref), custom_call_target="tpu_custom_call" | custom-call | tf_op jit(solution)/shard_map/pallas_call | solution.py:353
  89.7 0.0 all-to-all-done.1
  89.7 5.0 %shard_map.103.hy_ref = f32[128,512]{1,0:T(8,128)} custom-call(s32[32]{0:T(128)} %place_ref.9, s32[32,128]{1,0:T(8,128)} %bitcast.14, f32[3,7,512]{2,1,0:T(8,128)} %get-tuple-element.22.short_ref, f32[128,512]{1,0:T(8,128)} %get-tuple-element.24.t_ref, f32[128,512]{1,0:T(8,128)} %get-tuple-element.25.f0_ref, f32[128,512]{1,0:T(8,128)} %get-tuple-element.26.own_ref, ...), custom_call_target="tpu_custom_call" | custom-call | tf_op jit(solution)/shard_map/pallas_call | solution.py:394
  94.7 0.0 collective-permute-done.17.a1
  94.7 0.0 collective-permute-done.18.a2
  94.7 0.0 collective-permute-done.19.a3
  94.7 1.9 %shard_map.106 = (f32[128,512]{1,0:T(8,128)}, f32[8,128]{1,0:T(8,128)}) custom-call(f32[128,512]{1,0:T(8,128)} %shard_map.103.hy_ref, f32[128,128]{1,0:T(8,128)} %get-tuple-element.33.a0, f32[128,128]{1,0:T(8,128)S(1)} %collective-permute-done.17.a1, f32[128,128]{1,0:T(8,128)S(1)} %collective-permute-done.18.a2, f32[128,128]{1,0:T(8,128)S(1)} %collective-permute-done.19.a3), custom_call_target="tpu_custom_call" | custom-call | tf_op jit(solution)/shard_map/pallas_call | solution.py:397
  96.7 3.0 %collective-permute-start.22 = (f32[8,128]{1,0:T(8,128)}, f32[8,128]{1,0:T(8,128)S(1)}, u32[]{:S(2)}, u32[]{:S(2)}) collective-permute-start(f32[8,128]{1,0:T(8,128)} %get-tuple-element.38), channel_id=1, source_target_pairs={{0,6},{1,7},{2,0},{3,1},{4,2},{5,3},{6,4},{7,5},{8,14},{9,15},{10,... | collective-permute-start | bytes 12296 | tf_op jit(solution)/shard_map/ppermute | solution.py:400
  99.7 2.2 %collective-permute-start.20 = (f32[8,128]{1,0:T(8,128)}, f32[8,128]{1,0:T(8,128)S(1)}, u32[]{:S(2)}, u32[]{:S(2)}) collective-permute-start(f32[8,128]{1,0:T(8,128)} %get-tuple-element.38), channel_id=1, source_target_pairs={{0,4},{1,5},{2,6},{3,7},{4,0},{5,1},{6,2},{7,3},{8,12},{9,13},{10,... | collective-permute-start | bytes 12296 | tf_op jit(solution)/shard_map/ppermute | solution.py:400
  101.9 0.0 collective-permute-done.22
  101.9 2.8 %collective-permute-done.21 = f32[8,128]{1,0:T(8,128)S(1)} collective-permute-done((f32[8,128]{1,0:T(8,128)}, f32[8,128]{1,0:T(8,128)S(1)}, u32[]{:S(2)}, u32[]{:S(2)}) %collective-permute-start.21) | collective-permute-done | bytes 4128 | tf_op jit(solution)/shard_map/ppermute | solution.py:400
  104.7 0.3 collective-permute-done.20
  105.0 0.7 add_add_fusion.sq_ref
  105.7 2.1 %collective-permute-start.23 = (f32[8,128]{1,0:T(8,128)S(1)}, f32[8,128]{1,0:T(8,128)S(1)}, u32[]{:S(2)}, u32[]{:S(2)}) collective-permute-start(f32[8,128]{1,0:T(8,128)S(1)} %add_add_fusion.sq_ref), channel_id=1, source_target_pairs={{0,1},{1,0},{2,3},{3,2},{4,5},{5,4},{6,7},{7,6},{8,9},{9,8},{10,11... | collective-permute-start | bytes 12296 | tf_op jit(solution)/shard_map/ppermute | solution.py:337
  107.8 3.0 %collective-permute-done.23.other_ref = f32[8,128]{1,0:T(8,128)S(1)} collective-permute-done((f32[8,128]{1,0:T(8,128)S(1)}, f32[8,128]{1,0:T(8,128)S(1)}, u32[]{:S(2)}, u32[]{:S(2)}) %collective-permute-start.23) | collective-permute-done | bytes 4128 | tf_op jit(solution)/shard_map/ppermute | solution.py:337
  110.8 1.8 %shard_map.107 = f32[128,512]{1,0:T(8,128)} custom-call(f32[128,512]{1,0:T(8,128)} %get-tuple-element.37.y_ref, f32[8,128]{1,0:T(8,128)} %copy-done.16, f32[8,128]{1,0:T(8,128)S(1)} %collective-permute-done.23.other_ref, f32[1,512]{1,0:T(1,128)} %bitcast.17), custom_call_target="tpu_custom_call" | custom-call | tf_op jit(solution)/shard_map/pallas_call | solution.py:404
  (37 shorter events, 0.1 us)
Async XLA Ops:
  2.1 18.8 %collective-permute-start = (f32[3,128,128]{2,1,0:T(8,128)}, f32[3,128,128]{2,1,0:T(8,128)S(1)}, u32[]{:S(2)}, u32[]{:S(2)}) collective-permute-start(f32[3,128,128]{2,1,0:T(8,128)} %get-tuple-element.30), channel_id=1, source_target_pairs={{0,64},{8,72},{16,80},{24,88},{32,96},{40,104},{48,112},{56,120},{... | collective-permute-start | bytes 589832 | tf_op jit(solution)/shard_map/ppermute | solution.py:334
  5.4 17.3 %collective-permute-start.1 = (f32[3,128,128]{2,1,0:T(8,128)}, f32[3,128,128]{2,1,0:T(8,128)S(1)}, u32[]{:S(2)}, u32[]{:S(2)}) collective-permute-start(f32[3,128,128]{2,1,0:T(8,128)} %get-tuple-element.31), channel_id=1, source_target_pairs={{0,128},{8,136},{16,144},{24,152},{32,160},{40,168},{48,176},{56,1... | collective-permute-start | bytes 589832 | tf_op jit(solution)/shard_map/ppermute | solution.py:334
  10.8 19.9 %collective-permute-start.2 = (f32[3,128,128]{2,1,0:T(8,128)}, f32[3,128,128]{2,1,0:T(8,128)S(1)}, u32[]{:S(2)}, u32[]{:S(2)}) collective-permute-start(f32[3,128,128]{2,1,0:T(8,128)} %get-tuple-element.32), channel_id=1, source_target_pairs={{0,192},{8,200},{16,208},{24,216},{32,224},{40,232},{48,240},{56,2... | collective-permute-start | bytes 589832 | tf_op jit(solution)/shard_map/ppermute | solution.py:334
  16.7 4.2 %copy-start.2 = (f32[3,128,128]{2,1,0:T(8,128)S(1)}, f32[3,128,128]{2,1,0:T(8,128)}, u32[]{:S(2)}) copy-start(f32[3,128,128]{2,1,0:T(8,128)} %get-tuple-element.29.a0) | copy-start | bytes 589828
  16.7 22.0 %all-to-all-start = ((f32[32,24,128]{2,1,0:T(8,128)}), f32[32,24,128]{2,1,0:T(8,128)S(1)}, u32[]{:S(2)}, u32[]{:S(2)}) async-start(f32[32,24,128]{2,1,0:T(8,128)} %bitcast.10), calls=%async_computation | async-start | bytes 786432 | tf_op jit(solution)/shard_map/all_to_all | solution.py:350
  20.9 1.8 %copy-start.3 = (f32[3,128,128]{2,1,0:T(8,128)}, f32[3,128,128]{2,1,0:T(8,128)S(1)}, u32[]{:S(2)}) copy-start(f32[3,128,128]{2,1,0:T(8,128)S(1)} %collective-permute-done.a1) | copy-start | bytes 589828
  22.7 8.0 %copy-start.4 = (f32[3,128,128]{2,1,0:T(8,128)}, f32[3,128,128]{2,1,0:T(8,128)S(1)}, u32[]{:S(2)}) copy-start(f32[3,128,128]{2,1,0:T(8,128)S(1)} %collective-permute-done.1.a2) | copy-start | bytes 589828
  30.7 0.7 copy-start.5
  31.4 0.7 copy-start
  31.4 17.9 %collective-permute-start.8 = (f32[4,128,128]{2,1,0:T(8,128)S(1)}, f32[4,128,128]{2,1,0:T(8,128)S(1)}, u32[]{:S(2)}, u32[]{:S(2)}) collective-permute-start(f32[4,128,128]{2,1,0:T(8,128)S(1)} %pad_maximum_fusion.rest_0_), channel_id=1, source_target_pairs={{0,32},{8,40},{16,48},{24,56},{32,0},{40,8},{48,16},{56,24},{64,96... | collective-permute-start | bytes 786440 | tf_op jit(solution)/shard_map/ppermute | solution.py:337
  31.4 18.0 %collective-permute-start.5 = (f32[4,128,128]{2,1,0:T(8,128)S(1)}, f32[4,128,128]{2,1,0:T(8,128)S(1)}, u32[]{:S(2)}, u32[]{:S(2)}) collective-permute-start(f32[4,128,128]{2,1,0:T(8,128)S(1)} %pad_maximum_fusion.rest_0_), channel_id=1, source_target_pairs={{0,16},{8,24},{16,0},{24,8},{32,48},{40,56},{48,32},{56,40},{64,80... | collective-permute-start | bytes 786440 | tf_op jit(solution)/shard_map/ppermute | solution.py:337
  31.8 18.3 %collective-permute-start.3 = (f32[4,128,128]{2,1,0:T(8,128)S(1)}, f32[4,128,128]{2,1,0:T(8,128)S(1)}, u32[]{:S(2)}, u32[]{:S(2)}) collective-permute-start(f32[4,128,128]{2,1,0:T(8,128)S(1)} %pad_maximum_fusion.rest_0_), channel_id=1, source_target_pairs={{0,8},{8,0},{16,24},{24,16},{32,40},{40,32},{48,56},{56,48},{64,72... | collective-permute-start | bytes 786440 | tf_op jit(solution)/shard_map/ppermute | solution.py:337
  32.1 17.2 %copy-start.1 = (f32[4,128,128]{2,1,0:T(8,128)}, f32[4,128,128]{2,1,0:T(8,128)S(1)}, u32[]{:S(2)}) copy-start(f32[4,128,128]{2,1,0:T(8,128)S(1)} %pad_maximum_fusion.1.rest_1_) | copy-start | bytes 786436
  32.1 18.1 %collective-permute-start.6 = (f32[4,128,128]{2,1,0:T(8,128)S(1)}, f32[4,128,128]{2,1,0:T(8,128)S(1)}, u32[]{:S(2)}, u32[]{:S(2)}) collective-permute-start(f32[4,128,128]{2,1,0:T(8,128)S(1)} %pad_maximum_fusion.1.rest_1_), channel_id=1, source_target_pairs={{0,16},{8,24},{16,0},{24,8},{32,48},{40,56},{48,32},{56,40},{64,80... | collective-permute-start | bytes 786440 | tf_op jit(solution)/shard_map/ppermute | solution.py:337
  40.3 49.4 %all-to-all-start.1 = ((f32[32,24,128]{2,1,0:T(8,128)}), f32[32,24,128]{2,1,0:T(8,128)S(1)}, u32[]{:S(2)}, u32[]{:S(2)}) async-start(f32[32,24,128]{2,1,0:T(8,128)} %shard_map.102), calls=%async_computation.1 | async-start | bytes 786432 | tf_op jit(solution)/shard_map/all_to_all | solution.py:370
  47.7 17.1 %collective-permute-start.9 = (f32[4,128,128]{2,1,0:T(8,128)S(1)}, f32[4,128,128]{2,1,0:T(8,128)S(1)}, u32[]{:S(2)}, u32[]{:S(2)}) collective-permute-start(f32[4,128,128]{2,1,0:T(8,128)S(1)} %pad_maximum_fusion.1.rest_1_), channel_id=1, source_target_pairs={{0,32},{8,40},{16,48},{24,56},{32,0},{40,8},{48,16},{56,24},{64,96... | collective-permute-start | bytes 786440 | tf_op jit(solution)/shard_map/ppermute | solution.py:337
  49.3 22.2 %copy-start.6 = (f32[4,128,128]{2,1,0:T(8,128)}, f32[4,128,128]{2,1,0:T(8,128)S(1)}, u32[]{:S(2)}) copy-start(f32[4,128,128]{2,1,0:T(8,128)S(1)} %collective-permute-done.8.rest_7_) | copy-start | bytes 786436
  49.3 15.6 %collective-permute-start.4 = (f32[4,128,128]{2,1,0:T(8,128)S(1)}, f32[4,128,128]{2,1,0:T(8,128)S(1)}, u32[]{:S(2)}, u32[]{:S(2)}) collective-permute-start(f32[4,128,128]{2,1,0:T(8,128)S(1)} %pad_maximum_fusion.1.rest_1_), channel_id=1, source_target_pairs={{0,8},{8,0},{16,24},{24,16},{32,40},{40,32},{48,56},{56,48},{64,72... | collective-permute-start | bytes 786440 | tf_op jit(solution)/shard_map/ppermute | solution.py:337
  49.4 22.1 %copy-start.7 = (f32[4,128,128]{2,1,0:T(8,128)}, f32[4,128,128]{2,1,0:T(8,128)S(1)}, u32[]{:S(2)}) copy-start(f32[4,128,128]{2,1,0:T(8,128)S(1)} %collective-permute-done.5.rest_4_) | copy-start | bytes 786436
  49.4 16.0 %collective-permute-start.11 = (f32[4,128,128]{2,1,0:T(8,128)S(1)}, f32[4,128,128]{2,1,0:T(8,128)S(1)}, u32[]{:S(2)}, u32[]{:S(2)}) collective-permute-start(f32[4,128,128]{2,1,0:T(8,128)S(1)} %collective-permute-done.8.rest_7_), channel_id=1, source_target_pairs={{0,16},{8,24},{16,0},{24,8},{32,48},{40,56},{48,32},{56,40},{64,80... | collective-permute-start | bytes 786440 | tf_op jit(solution)/shard_map/ppermute | solution.py:337
  50.0 21.4 %copy-start.8 = (f32[4,128,128]{2,1,0:T(8,128)}, f32[4,128,128]{2,1,0:T(8,128)S(1)}, u32[]{:S(2)}) copy-start(f32[4,128,128]{2,1,0:T(8,128)S(1)} %collective-permute-done.3.rest_2_) | copy-start | bytes 786436
  50.0 15.4 %collective-permute-start.10 = (f32[4,128,128]{2,1,0:T(8,128)S(1)}, f32[4,128,128]{2,1,0:T(8,128)S(1)}, u32[]{:S(2)}, u32[]{:S(2)}) collective-permute-start(f32[4,128,128]{2,1,0:T(8,128)S(1)} %collective-permute-done.8.rest_7_), channel_id=1, source_target_pairs={{0,8},{8,0},{16,24},{24,16},{32,40},{40,32},{48,56},{56,48},{64,72... | collective-permute-start | bytes 786440 | tf_op jit(solution)/shard_map/ppermute | solution.py:337
  50.2 21.3 %copy-start.9 = (f32[4,128,128]{2,1,0:T(8,128)}, f32[4,128,128]{2,1,0:T(8,128)S(1)}, u32[]{:S(2)}) copy-start(f32[4,128,128]{2,1,0:T(8,128)S(1)} %collective-permute-done.6.rest_5_) | copy-start | bytes 786436
  50.2 19.7 %collective-permute-start.12 = (f32[4,128,128]{2,1,0:T(8,128)S(1)}, f32[4,128,128]{2,1,0:T(8,128)S(1)}, u32[]{:S(2)}, u32[]{:S(2)}) collective-permute-start(f32[4,128,128]{2,1,0:T(8,128)S(1)} %collective-permute-done.6.rest_5_), channel_id=1, source_target_pairs={{0,32},{8,40},{16,48},{24,56},{32,0},{40,8},{48,16},{56,24},{64,96... | collective-permute-start | bytes 786440 | tf_op jit(solution)/shard_map/ppermute | solution.py:337
  64.8 6.6 %copy-start.10 = (f32[4,128,128]{2,1,0:T(8,128)}, f32[4,128,128]{2,1,0:T(8,128)S(1)}, u32[]{:S(2)}) copy-start(f32[4,128,128]{2,1,0:T(8,128)S(1)} %collective-permute-done.9.rest_8_) | copy-start | bytes 786436
  64.8 5.1 %collective-permute-start.7 = (f32[4,128,128]{2,1,0:T(8,128)S(1)}, f32[4,128,128]{2,1,0:T(8,128)S(1)}, u32[]{:S(2)}, u32[]{:S(2)}) collective-permute-start(f32[4,128,128]{2,1,0:T(8,128)S(1)} %collective-permute-done.6.rest_5_), channel_id=1, source_target_pairs={{0,8},{8,0},{16,24},{24,16},{32,40},{40,32},{48,56},{56,48},{64,72... | collective-permute-start | bytes 786440 | tf_op jit(solution)/shard_map/ppermute | solution.py:337
  64.9 6.6 %copy-start.11 = (f32[4,128,128]{2,1,0:T(8,128)}, f32[4,128,128]{2,1,0:T(8,128)S(1)}, u32[]{:S(2)}) copy-start(f32[4,128,128]{2,1,0:T(8,128)S(1)} %collective-permute-done.4.rest_3_) | copy-start | bytes 786436
  64.9 5.0 %collective-permute-start.13 = (f32[4,128,128]{2,1,0:T(8,128)S(1)}, f32[4,128,128]{2,1,0:T(8,128)S(1)}, u32[]{:S(2)}, u32[]{:S(2)}) collective-permute-start(f32[4,128,128]{2,1,0:T(8,128)S(1)} %collective-permute-done.5.rest_4_), channel_id=1, source_target_pairs={{0,8},{8,0},{16,24},{24,16},{32,40},{40,32},{48,56},{56,48},{64,72... | collective-permute-start | bytes 786440 | tf_op jit(solution)/shard_map/ppermute | solution.py:337
  65.4 6.1 %copy-start.12 = (f32[4,128,128]{2,1,0:T(8,128)}, f32[4,128,128]{2,1,0:T(8,128)S(1)}, u32[]{:S(2)}) copy-start(f32[4,128,128]{2,1,0:T(8,128)S(1)} %collective-permute-done.11.rest_10_) | copy-start | bytes 786436
  65.4 4.5 %collective-permute-start.14 = (f32[4,128,128]{2,1,0:T(8,128)S(1)}, f32[4,128,128]{2,1,0:T(8,128)S(1)}, u32[]{:S(2)}, u32[]{:S(2)}) collective-permute-start(f32[4,128,128]{2,1,0:T(8,128)S(1)} %collective-permute-done.9.rest_8_), channel_id=1, source_target_pairs={{0,8},{8,0},{16,24},{24,16},{32,40},{40,32},{48,56},{56,48},{64,72... | collective-permute-start | bytes 786440 | tf_op jit(solution)/shard_map/ppermute | solution.py:337
  65.5 6.0 %copy-start.13 = (f32[4,128,128]{2,1,0:T(8,128)}, f32[4,128,128]{2,1,0:T(8,128)S(1)}, u32[]{:S(2)}) copy-start(f32[4,128,128]{2,1,0:T(8,128)S(1)} %collective-permute-done.10.rest_9_) | copy-start | bytes 786436
  65.5 4.5 %collective-permute-start.15 = (f32[4,128,128]{2,1,0:T(8,128)S(1)}, f32[4,128,128]{2,1,0:T(8,128)S(1)}, u32[]{:S(2)}, u32[]{:S(2)}) collective-permute-start(f32[4,128,128]{2,1,0:T(8,128)S(1)} %collective-permute-done.11.rest_10_), channel_id=1, source_target_pairs={{0,8},{8,0},{16,24},{24,16},{32,40},{40,32},{48,56},{56,48},{64,72... | collective-permute-start | bytes 786440 | tf_op jit(solution)/shard_map/ppermute | solution.py:337
  69.9 0.7 copy-start.14
  69.9 1.5 %collective-permute-start.16 = (f32[4,128,128]{2,1,0:T(8,128)S(1)}, f32[4,128,128]{2,1,0:T(8,128)S(1)}, u32[]{:S(2)}, u32[]{:S(2)}) collective-permute-start(f32[4,128,128]{2,1,0:T(8,128)S(1)} %collective-permute-done.12.rest_11_), channel_id=1, source_target_pairs={{0,8},{8,0},{16,24},{24,16},{32,40},{40,32},{48,56},{56,48},{64,72... | collective-permute-start | bytes 786440 | tf_op jit(solution)/shard_map/ppermute | solution.py:337
  69.9 0.8 copy-start.15
  77.3 17.4 %collective-permute-start.17 = (f32[128,128]{1,0:T(8,128)}, f32[128,128]{1,0:T(8,128)S(1)}, u32[]{:S(2)}, u32[]{:S(2)}) collective-permute-start(f32[128,128]{1,0:T(8,128)} %get-tuple-element.34), channel_id=1, source_target_pairs={{0,192},{8,200},{16,208},{24,216},{32,224},{40,232},{48,240},{56,2... | collective-permute-start | bytes 196616 | tf_op jit(solution)/shard_map/ppermute | solution.py:334
  80.1 14.7 %collective-permute-start.18 = (f32[128,128]{1,0:T(8,128)}, f32[128,128]{1,0:T(8,128)S(1)}, u32[]{:S(2)}, u32[]{:S(2)}) collective-permute-start(f32[128,128]{1,0:T(8,128)} %get-tuple-element.35), channel_id=1, source_target_pairs={{0,128},{8,136},{16,144},{24,152},{32,160},{40,168},{48,176},{56,1... | collective-permute-start | bytes 196616 | tf_op jit(solution)/shard_map/ppermute | solution.py:334
  83.3 11.4 %collective-permute-start.19 = (f32[128,128]{1,0:T(8,128)}, f32[128,128]{1,0:T(8,128)S(1)}, u32[]{:S(2)}, u32[]{:S(2)}) collective-permute-start(f32[128,128]{1,0:T(8,128)} %get-tuple-element.36), channel_id=1, source_target_pairs={{0,64},{8,72},{16,80},{24,88},{32,96},{40,104},{48,112},{56,120},{... | collective-permute-start | bytes 196616 | tf_op jit(solution)/shard_map/ppermute | solution.py:334
  96.7 5.2 %collective-permute-start.22 = (f32[8,128]{1,0:T(8,128)}, f32[8,128]{1,0:T(8,128)S(1)}, u32[]{:S(2)}, u32[]{:S(2)}) collective-permute-start(f32[8,128]{1,0:T(8,128)} %get-tuple-element.38), channel_id=1, source_target_pairs={{0,6},{1,7},{2,0},{3,1},{4,2},{5,3},{6,4},{7,5},{8,14},{9,15},{10,... | collective-permute-start | bytes 12296 | tf_op jit(solution)/shard_map/ppermute | solution.py:400
  99.7 5.0 %collective-permute-start.21 = (f32[8,128]{1,0:T(8,128)}, f32[8,128]{1,0:T(8,128)S(1)}, u32[]{:S(2)}, u32[]{:S(2)}) collective-permute-start(f32[8,128]{1,0:T(8,128)} %get-tuple-element.38), channel_id=1, source_target_pairs={{0,2},{1,3},{2,4},{3,5},{4,6},{5,7},{6,0},{7,1},{8,10},{9,11},{10,... | collective-permute-start | bytes 12296 | tf_op jit(solution)/shard_map/ppermute | solution.py:400
  99.7 5.3 %collective-permute-start.20 = (f32[8,128]{1,0:T(8,128)}, f32[8,128]{1,0:T(8,128)S(1)}, u32[]{:S(2)}, u32[]{:S(2)}) collective-permute-start(f32[8,128]{1,0:T(8,128)} %get-tuple-element.38), channel_id=1, source_target_pairs={{0,4},{1,5},{2,6},{3,7},{4,0},{5,1},{6,2},{7,3},{8,12},{9,13},{10,... | collective-permute-start | bytes 12296 | tf_op jit(solution)/shard_map/ppermute | solution.py:400
  105.7 5.1 %copy-start.16 = (f32[8,128]{1,0:T(8,128)}, f32[8,128]{1,0:T(8,128)S(1)}, u32[]{:S(2)}) copy-start(f32[8,128]{1,0:T(8,128)S(1)} %add_add_fusion.sq_ref) | copy-start | bytes 12292
  105.7 5.1 %collective-permute-start.23 = (f32[8,128]{1,0:T(8,128)S(1)}, f32[8,128]{1,0:T(8,128)S(1)}, u32[]{:S(2)}, u32[]{:S(2)}) collective-permute-start(f32[8,128]{1,0:T(8,128)S(1)} %add_add_fusion.sq_ref), channel_id=1, source_target_pairs={{0,1},{1,0},{2,3},{3,2},{4,5},{5,4},{6,7},{7,6},{8,9},{9,8},{10,11... | collective-permute-start | bytes 12296 | tf_op jit(solution)/shard_map/ppermute | solution.py:337
